TPU v7x, 32 devices: a whole 2x2x4 slice. The times are simulated.
32 devices in a mesh: prow: 8 (over z, core), pcol: 4 (over y, x).
Axes of the slice: x: 2, y: 2, z: 4, core: 2. Of those that a mesh axis runs over, the one named last changes fastest.
Arguments:
- trailing_in: float32 [2048, 2048], P('prow', 'pcol'), may hold values from -6 to 6
- panel_t: float32 [256, 2048], P('pcol', 'prow'), may hold values from -0.375 to 0.375
- pivots: int32 [256], replicated, may hold values from 0 to 2047, as said below
Outputs:
- trailing: float32 [2048, 2048], P('prow', 'pcol')
Inputs may be any that keep to these rules, and one draw needn't show every extreme that they name: pivots[k] is at least k and below 2048; one entry equals 2047.
All inputs are finite; a program needn't handle non-finite values.
Results may differ from a plain program's by a relative error of at most 0.000076.
Values sent between devices are 32-bit elements; how exact they have to be, the bound alone decides.
No kernel may reach another device: no remote copies, remote signals or barrier semaphores. Data moves between devices by JAX's collectives and lax.ppermute only.
A program may use at most 64 MiB of HBM per device.

v0:
```python
import functools

import jax
import jax.numpy as jnp
from jax import lax
from jax.experimental import pallas as pl
from jax.experimental.pallas import tpu as pltpu
from jax.sharding import PartitionSpec as P

VMEM = pl.BlockSpec(memory_space=pltpu.VMEM)
SMEM = pl.BlockSpec(memory_space=pltpu.SMEM)
ANY = pl.BlockSpec(memory_space=pl.ANY)
F32 = jnp.float32
UNROLL = 32


def pair_exchange(value, axis, bit):
    size = lax.axis_size(axis)
    return lax.ppermute(value, axis, [(i, i ^ bit) for i in range(size)])


def inside(rows, low, count):
    return (rows >= low) & (rows < low + count)


def pick_body(pivots, trailing, keep, send, slots, table, block, sem):
    width = pivots.shape[0]
    rows = trailing.shape[0]
    half = width // 2
    me = lax.axis_index("prow")
    core = lax.rem(me, 2)
    first = me * rows
    load = pltpu.make_async_copy(trailing, block, sem)
    load.start()

    def fill(i, _):
        for u in range(UNROLL):
            table[i * UNROLL + u] = i * UNROLL + u
        for u in range(UNROLL):
            pivot = pivots[i * UNROLL + u]
            table[pivot] = pivot
        return 0

    def exchange(i, _):
        for u in range(UNROLL):
            k = i * UNROLL + u
            pivot = pivots[k]
            mine = table[k]
            slots[k] = table[pivot]
            table[pivot] = mine
        return 0

    lax.fori_loop(0, width // UNROLL, fill, 0)
    lax.fori_loop(0, width // UNROLL, exchange, 0)
    load.wait()

    def pick(offset, target):
        def some(i, _):
            for u in range(UNROLL):
                j = i * UNROLL + u
                row = slots[offset + j]
                local = row - first
                own = (local >= 0) & (local < rows)
                index = jnp.where(own, local, jnp.where(me == 0, table[row], 0))
                target[pl.ds(j, 1), :] = block[pl.ds(index, 1), :]
            return 0

        lax.fori_loop(0, half // UNROLL, some, 0)

    pick((1 - core) * half, send)
    pick(core * half, keep)


def column_body(slots, column):
    def some(i, _):
        for u in range(UNROLL):
            j = i * UNROLL + u
            column[pl.ds(j, 1), :] = jnp.full((1, column.shape[1]), slots[j], jnp.int32)
        return 0

    lax.fori_loop(0, column.shape[0] // UNROLL, some, 0)


def chip_body(rows, keep, recv, column, *pieces):
    me = lax.axis_index("prow")
    chip, core = me // 2, lax.rem(me, 2)
    for d, piece in enumerate(pieces):
        part = lax.bitwise_xor(chip, d)
        ids = column[core * len(pieces) + part][:, 0:1]
        second = inside(ids, (2 * chip + 1) * rows, rows)
        piece[...] = jnp.where(second == (core == 1), keep[part], recv[part])


def owner_body(rows, count, column, *refs):
    pieces, outs = refs[:count], refs[count:]
    me = lax.axis_index("prow")
    chip, core = me // 2, lax.rem(me, 2)
    ids = column[core * count + chip][:, 0:1]
    holds = [inside(ids, lax.bitwise_xor(chip, d) * 2 * rows, 2 * rows) for d in range(count)]
    chosen = pieces[0][...]
    leaving = pieces[0][...]
    for d in range(1, count):
        value = pieces[d][...]
        chosen = jnp.where(holds[d], value, chosen)
        leaving = jnp.where(chip == d, value, leaving)
    for d in range(count):
        outs[d][...] = jnp.where(holds[d], leaving, chosen)


def share_body(rows, keep, recv, column, *refs):
    count = keep.shape[0]
    parts, (own, send) = refs[:count], refs[count:]
    me = lax.axis_index("prow")
    chip, core = me // 2, lax.rem(me, 2)
    for d in range(count):
        part = lax.bitwise_xor(chip, d)
        ids = column[core * count + part][:, 0:1]
        mine, theirs = keep[part], recv[part]
        second = inside(ids, (2 * chip + 1) * rows, rows)
        here = jnp.where(second == (core == 1), mine, theirs)
        there = jnp.where(second & (chip == 0), jnp.where(core == 0, mine, theirs), parts[d][...])
        own[part] = jnp.where(inside(ids, lax.bitwise_xor(me, 1) * rows, rows), here, there)
        send[part] = jnp.where(inside(ids, me * rows, rows), here, there)


def dot(a, b):
    return lax.dot(a, b, precision=lax.Precision.HIGHEST, preferred_element_type=F32)


def factor_body(count, column, trailing, *refs):
    diag, lower = refs[:count], refs[count : 2 * count]
    a_ref, sel_ref, base_ref, diag_t, lower_t = refs[2 * count :]
    depth = diag[0].shape[0]
    width = depth * count
    rows = trailing.shape[0]
    me = lax.axis_index("prow")
    mine = lax.axis_index("pcol")
    for d in range(count):
        at = pl.ds(pl.multiple_of(lax.bitwise_xor(mine, d) * depth, depth), depth)
        diag_t[at, :] = diag[d][...]
        lower_t[at, :] = lower[d][...]
    i = lax.broadcasted_iota(jnp.int32, (width, width), 0)
    j = lax.broadcasted_iota(jnp.int32, (width, width), 1)
    full = diag_t[...]
    inverse = (i == j).astype(F32)
    size = 1
    while size < width:
        cross = (i // size + 1 == j // size) & (lax.rem(i // size, 2) == 0)
        block = jnp.where(cross, full, 0.0)
        inverse = inverse - (block if size == 1 else dot(inverse, dot(block, inverse)))
        size *= 2
    minus = -dot(inverse, lower_t[...])
    a_ref[...] = jnp.where(me == 0, inverse, minus).T
    ids = column[...].astype(F32).T[0:1, :]
    own = (me * rows + lax.broadcasted_iota(jnp.int32, (rows, width), 0)).astype(F32)
    match = (ids == own) & (me > 0)
    sel = jnp.where(match, 1.0, 0.0)
    sel_ref[...] = sel.astype(jnp.bfloat16)
    drop = (jnp.max(sel, axis=1, keepdims=True) > 0.0) | (me == 0)
    base_ref[...] = jnp.where(drop, 0.0, trailing[...])


def finish_body(rows, column, keep, send, own, recv, a_ref, sel_ref, base, out):
    half = keep.shape[0]
    me = lax.axis_index("prow")
    core = lax.rem(me, 2)

    def part(start, picked, arrived):
        at = pl.ds(pl.multiple_of(start, half), half)
        ids = column[at, 0:1]
        value = arrived[...]
        chosen = jnp.where(inside(ids, me * rows, rows), picked[...], value)
        high = value.astype(jnp.bfloat16)
        rest = value - high.astype(F32)
        middle = rest.astype(jnp.bfloat16)
        low = (rest - middle.astype(F32)).astype(jnp.bfloat16)
        sel = sel_ref[:, at]
        total = dot(a_ref[:, at], chosen)
        for term in (low, middle, high):
            total += lax.dot(sel, term, preferred_element_type=F32)
        return total

    first = part(core * half, keep, own)
    out[...] = base[...] + first + part((1 - core) * half, send, recv)


def on_device(trailing_in, panel_t, pivots):
    rows, cols = trailing_in.shape
    width = pivots.shape[0]
    half = width // 2
    devices = lax.axis_size("prow")
    chips = devices // 2
    spread = lax.axis_size("pcol")
    size = half // chips
    depth = panel_t.shape[0]
    assert rows == width and size * chips == half and depth * spread == width

    def array(*shape, dtype=F32):
        return jax.ShapeDtypeStruct(shape, dtype)

    me = lax.axis_index("prow")
    diag = panel_t
    bit = devices // 2
    while bit:
        diag = jnp.where((me & bit) > 0, pair_exchange(diag, "prow", bit), diag)
        bit //= 2
    lowers = [panel_t] + [pair_exchange(panel_t, "pcol", d) for d in range(1, spread)]
    diags = [diag] + [pair_exchange(diag, "pcol", d) for d in range(1, spread)]

    keep, send, slots = pl.pallas_call(
        pick_body,
        out_shape=(array(half, cols), array(half, cols), array(width, dtype=jnp.int32)),
        in_specs=[SMEM, ANY],
        out_specs=(VMEM, VMEM, SMEM),
        scratch_shapes=[
            pltpu.SMEM((rows * devices,), jnp.int32),
            pltpu.VMEM((rows, cols), F32),
            pltpu.SemaphoreType.DMA,
        ],
        name="pick",
    )(pivots, trailing_in)
    column = pl.pallas_call(
        column_body,
        out_shape=array(width, 128, dtype=jnp.int32),
        in_specs=[SMEM],
        out_specs=VMEM,
        name="column",
    )(slots)
    recv = pair_exchange(send, "prow", 1).reshape(chips, size, cols)
    cut = keep.reshape(chips, size, cols)
    ids = column.reshape(devices, size, 128)
    pieces = pl.pallas_call(
        functools.partial(chip_body, rows),
        out_shape=[array(size, cols)] * chips,
        in_specs=[VMEM] * 3,
        out_specs=[VMEM] * chips,
        name="chip",
    )(cut, recv, ids)
    gathered = [pieces[0]] + [pair_exchange(pieces[d], "prow", 2 * d) for d in range(1, chips)]
    parts = pl.pallas_call(
        functools.partial(owner_body, rows, chips),
        out_shape=[array(size, cols)] * chips,
        in_specs=[VMEM] * (1 + chips),
        out_specs=[VMEM] * chips,
        name="owner",
    )(ids, *gathered)
    parts = [parts[0]] + [pair_exchange(parts[d], "prow", 2 * d) for d in range(1, chips)]
    own, other = pl.pallas_call(
        functools.partial(share_body, rows),
        out_shape=[array(chips, size, cols)] * 2,
        in_specs=[VMEM] * (3 + chips),
        out_specs=[VMEM] * 2,
        name="share",
    )(cut, recv, ids, *parts)
    own = own.reshape(half, cols)
    arrived = pair_exchange(other, "prow", 1).reshape(half, cols)
    a, sel, base = pl.pallas_call(
        functools.partial(factor_body, spread),
        out_shape=(array(rows, width), array(rows, width, dtype=jnp.bfloat16), array(rows, cols)),
        in_specs=[VMEM] * (2 + 2 * spread),
        out_specs=(VMEM,) * 3,
        scratch_shapes=[pltpu.VMEM((width, width), F32), pltpu.VMEM((width, rows), F32)],
        name="factor",
    )(column, trailing_in, *diags, *lowers)
    return pl.pallas_call(
        functools.partial(finish_body, rows),
        out_shape=array(rows, cols),
        in_specs=[VMEM] * 8,
        out_specs=VMEM,
        name="finish",
    )(column, keep, send, own, arrived, a, sel, base)


def solution(mesh):
    in_specs = (P("prow", "pcol"), P("pcol", "prow"), P())
    out_specs = P("prow", "pcol")
    return jax.shard_map(
        on_device, mesh=mesh, in_specs=in_specs, out_specs=out_specs, check_vma=False
    )
```

profile of v0, /device:TPU:0, one launch (start us, length us, event | category | flops | bytes accessed | tf_op | source)
XLA Modules:
  0.0 61.2 jit_solution(10379130402009417368)
XLA Ops:
  0.0 4.6 %pick.1 = (f32[128,512]{1,0:T(8,128)}, f32[128,512]{1,0:T(8,128)}, s32[256]{0:T(256)}) custom-call(s32[256]{0:T(256)} %pivots.1, f32[256,512]{1,0:T(8,128)} %trailing.3), custom_call_target="tpu_custom_call" | custom-call | tf_op jit(solution)/shard_map/pick/pallas_call | solution.py:210
  5.2 3.7 %collective-permute-start.8 = (f32[64,256]{1,0:T(8,128)S(1)}, f32[64,256]{1,0:T(8,128)S(1)}, u32[]{:S(2)}, u32[]{:S(2)}) collective-permute-start(f32[64,256]{1,0:T(8,128)S(1)} %copy-done.2), channel_id=1, source_target_pairs={{0,16},{4,20},{8,24},{12,28},{16,0},{20,4},{24,8},{28,12},{1,17},{... | collective-permute-start | bytes 196616 | tf_op jit(solution)/shard_map/ppermute | solution.py:19
  8.8 1.5 %column.1 = s32[256,128]{1,0:T(8,128)} custom-call(s32[256]{0:T(256)} %get-tuple-element.21.slots), custom_call_target="tpu_custom_call" | custom-call | tf_op jit(solution)/shard_map/column/pallas_call | solution.py:222
  10.3 0.7 %copy-done = f32[128,512]{1,0:T(8,128)} copy-done((f32[128,512]{1,0:T(8,128)}, f32[128,512]{1,0:T(8,128)S(1)}, u32[]{:S(2)}) %copy-start) | copy-done | bytes 262168
  11.0 1.8 %chip.1 = (f32[32,512]{1,0:T(8,128)}, f32[32,512]{1,0:T(8,128)}, f32[32,512]{1,0:T(8,128)}, f32[32,512]{1,0:T(8,128)}) custom-call(f32[4,32,512]{2,1,0:T(8,128)} %bitcast.8, f32[4,32,512]{2,1,0:T(8,128)} %bitcast.10, s32[8,32,128]{2,1,0:T(8,128)} %bitcast.5), custom_call_target="tpu_custom_call" | custom-call | tf_op jit(solution)/shard_map/chip/pallas_call | solution.py:232
  12.9 1.6 %collective-permute-start.1 = (f32[32,512]{1,0:T(8,128)}, f32[32,512]{1,0:T(8,128)S(1)}, u32[]{:S(2)}, u32[]{:S(2)}) collective-permute-start(f32[32,512]{1,0:T(8,128)} %get-tuple-element.25), channel_id=1, source_target_pairs={{0,8},{4,12},{8,0},{12,4},{16,24},{20,28},{24,16},{28,20},{1,9},{5... | collective-permute-start | bytes 196616 | tf_op jit(solution)/shard_map/ppermute | solution.py:19
  14.8 2.5 %collective-permute-start.3 = (f32[32,512]{1,0:T(8,128)}, f32[32,512]{1,0:T(8,128)S(1)}, u32[]{:S(2)}, u32[]{:S(2)}) collective-permute-start(f32[32,512]{1,0:T(8,128)} %get-tuple-element.27), channel_id=1, source_target_pairs={{0,24},{4,28},{8,16},{12,20},{16,8},{20,12},{24,0},{28,4},{1,25},{... | collective-permute-start | bytes 196616 | tf_op jit(solution)/shard_map/ppermute | solution.py:19
  17.3 0.7 %collective-permute-start.9 = (f32[64,256]{1,0:T(8,128)S(1)}, f32[64,256]{1,0:T(8,128)S(1)}, u32[]{:S(2)}, u32[]{:S(2)}) collective-permute-start(f32[64,256]{1,0:T(8,128)S(1)} %broadcast_select_fusion), channel_id=1, source_target_pairs={{0,8},{4,12},{8,0},{12,4},{16,24},{20,28},{24,16},{28,20},{1,9},{5... | collective-permute-start | bytes 196616 | tf_op jit(solution)/shard_map/ppermute | solution.py:19
  18.0 4.5 %collective-permute-done.2.refs_2_ = f32[32,512]{1,0:T(8,128)S(1)} collective-permute-done((f32[32,512]{1,0:T(8,128)}, f32[32,512]{1,0:T(8,128)S(1)}, u32[]{:S(2)}, u32[]{:S(2)}) %collective-permute-start.2) | collective-permute-done | bytes 65568 | tf_op jit(solution)/shard_map/ppermute | solution.py:19
  23.2 1.8 %owner.1 = (f32[32,512]{1,0:T(8,128)}, f32[32,512]{1,0:T(8,128)}, f32[32,512]{1,0:T(8,128)}, f32[32,512]{1,0:T(8,128)}) custom-call(s32[8,32,128]{2,1,0:T(8,128)} %bitcast.6, f32[32,512]{1,0:T(8,128)} %get-tuple-element.24.refs_0_, f32[32,512]{1,0:T(8,128)} %copy-done.13, f32[32,512]{1,0:T(8,128)} %copy-done.14, f32[32,512]{1,0:T(8,128)} %copy-done.15), custom_call_target="tpu_custom_call" | custom-call | tf_op jit(solution)/shard_map/owner/pallas_call | solution.py:240
  25.0 1.6 %collective-permute-start.4 = (f32[32,512]{1,0:T(8,128)}, f32[32,512]{1,0:T(8,128)S(1)}, u32[]{:S(2)}, u32[]{:S(2)}) collective-permute-start(f32[32,512]{1,0:T(8,128)} %get-tuple-element.29), channel_id=1, source_target_pairs={{0,8},{4,12},{8,0},{12,4},{16,24},{20,28},{24,16},{28,20},{1,9},{5... | collective-permute-start | bytes 196616 | tf_op jit(solution)/shard_map/ppermute | solution.py:19
  27.1 2.2 %collective-permute-start.6 = (f32[32,512]{1,0:T(8,128)}, f32[32,512]{1,0:T(8,128)S(1)}, u32[]{:S(2)}, u32[]{:S(2)}) collective-permute-start(f32[32,512]{1,0:T(8,128)} %get-tuple-element.31), channel_id=1, source_target_pairs={{0,24},{4,28},{8,16},{12,20},{16,8},{20,12},{24,0},{28,4},{1,25},{... | collective-permute-start | bytes 196616 | tf_op jit(solution)/shard_map/ppermute | solution.py:19
  29.5 1.6 %collective-permute-start.15 = (f32[64,256]{1,0:T(8,128)S(1)}, f32[64,256]{1,0:T(8,128)S(1)}, u32[]{:S(2)}, u32[]{:S(2)}) collective-permute-start(f32[64,256]{1,0:T(8,128)S(1)} %copy-done.2), channel_id=1, source_target_pairs={{0,2},{1,3},{2,0},{3,1},{4,6},{5,7},{6,4},{7,5},{8,10},{9,11},{10,... | collective-permute-start | bytes 196616 | tf_op jit(solution)/shard_map/ppermute | solution.py:19
  31.0 1.5 %collective-permute-start.14 = (f32[64,256]{1,0:T(8,128)S(1)}, f32[64,256]{1,0:T(8,128)S(1)}, u32[]{:S(2)}, u32[]{:S(2)}) collective-permute-start(f32[64,256]{1,0:T(8,128)S(1)} %copy-done.2), channel_id=1, source_target_pairs={{0,1},{1,0},{2,3},{3,2},{4,5},{5,4},{6,7},{7,6},{8,9},{9,8},{10,11... | collective-permute-start | bytes 196616 | tf_op jit(solution)/shard_map/ppermute | solution.py:19
  32.5 1.6 %collective-permute-done.5.refs_2_ = f32[32,512]{1,0:T(8,128)S(1)} collective-permute-done((f32[32,512]{1,0:T(8,128)}, f32[32,512]{1,0:T(8,128)S(1)}, u32[]{:S(2)}, u32[]{:S(2)}) %collective-permute-start.5) | collective-permute-done | bytes 65568 | tf_op jit(solution)/shard_map/ppermute | solution.py:19
  34.2 2.4 %collective-permute-start.16 = (f32[64,256]{1,0:T(8,128)S(1)}, f32[64,256]{1,0:T(8,128)S(1)}, u32[]{:S(2)}, u32[]{:S(2)}) collective-permute-start(f32[64,256]{1,0:T(8,128)S(1)} %copy-done.2), channel_id=1, source_target_pairs={{0,3},{1,2},{2,1},{3,0},{4,7},{5,6},{6,5},{7,4},{8,11},{9,10},{10,... | collective-permute-start | bytes 196616 | tf_op jit(solution)/shard_map/ppermute | solution.py:19
  36.6 0.6 %copy-done.6 = f32[32,512]{1,0:T(8,128)} copy-done((f32[32,512]{1,0:T(8,128)}, f32[32,512]{1,0:T(8,128)S(1)}, u32[]{:S(2)}) %copy-start.6) | copy-done | bytes 65560
  37.2 2.1 %share.1 = (f32[4,32,512]{2,1,0:T(8,128)}, f32[4,32,512]{2,1,0:T(8,128)}) custom-call(f32[4,32,512]{2,1,0:T(8,128)} %bitcast.9, f32[4,32,512]{2,1,0:T(8,128)} %bitcast.11, s32[8,32,128]{2,1,0:T(8,128)} %bitcast.7, f32[32,512]{1,0:T(8,128)} %get-tuple-element.28.refs_0_, f32[32,512]{1,0:T(8,128)} %copy-done.4, f32[32,512]{1,0:T(8,128)} %copy-done.5, ...), custom_call_target="tpu_custom_call" | custom-call | tf_op jit(solution)/shard_map/share/pallas_call | solution.py:248
  39.9 1.5 %collective-permute-start.12 = (f32[64,256]{1,0:T(8,128)S(1)}, f32[64,256]{1,0:T(8,128)S(1)}, u32[]{:S(2)}, u32[]{:S(2)}) collective-permute-start(f32[64,256]{1,0:T(8,128)S(1)} %broadcast_select_fusion.2.refs_0_), channel_id=1, source_target_pairs={{0,2},{1,3},{2,0},{3,1},{4,6},{5,7},{6,4},{7,5},{8,10},{9,11},{10,... | collective-permute-start | bytes 196616 | tf_op jit(solution)/shard_map/ppermute | solution.py:19
  41.4 1.5 %collective-permute-start.11 = (f32[64,256]{1,0:T(8,128)S(1)}, f32[64,256]{1,0:T(8,128)S(1)}, u32[]{:S(2)}, u32[]{:S(2)}) collective-permute-start(f32[64,256]{1,0:T(8,128)S(1)} %broadcast_select_fusion.2.refs_0_), channel_id=1, source_target_pairs={{0,1},{1,0},{2,3},{3,2},{4,5},{5,4},{6,7},{7,6},{8,9},{9,8},{10,11... | collective-permute-start | bytes 196616 | tf_op jit(solution)/shard_map/ppermute | solution.py:19
  42.9 2.4 %collective-permute-done.13.refs_3_ = f32[64,256]{1,0:T(8,128)S(1)} collective-permute-done((f32[64,256]{1,0:T(8,128)S(1)}, f32[64,256]{1,0:T(8,128)S(1)}, u32[]{:S(2)}, u32[]{:S(2)}) %collective-permute-start.13) | collective-permute-done | bytes 65568 | tf_op jit(solution)/shard_map/ppermute | solution.py:19
  46.8 9.9 %factor.1 = (f32[256,256]{1,0:T(8,128)}, bf16[256,256]{1,0:T(8,128)(2,1)}, f32[256,512]{1,0:T(8,128)}) custom-call(s32[256,128]{1,0:T(8,128)} %column.1, f32[256,512]{1,0:T(8,128)} %trailing.3, f32[64,256]{1,0:T(8,128)} %copy-done.3, f32[64,256]{1,0:T(8,128)} %copy-done.12, f32[64,256]{1,0:T(8,128)} %copy-done.11, f32[64,256]{1,0:T(8,128)} %copy-done.10, ...), custom_call_target="tpu_custom_call" | custom-call | tf_op jit(solution)/shard_map/factor/pallas_call | solution.py:257
  56.7 0.7 %copy-done.1 = f32[4,32,512]{2,1,0:T(8,128)} copy-done((f32[4,32,512]{2,1,0:T(8,128)}, f32[4,32,512]{2,1,0:T(8,128)S(1)}, u32[]{:S(2)}) %copy-start.1) | copy-done | bytes 262168
  57.4 3.8 %finish.1 = f32[256,512]{1,0:T(8,128)} custom-call(s32[256,128]{1,0:T(8,128)} %column.1, f32[128,512]{1,0:T(8,128)} %get-tuple-element.22.keep, f32[128,512]{1,0:T(8,128)} %get-tuple-element.23.send, f32[128,512]{1,0:T(8,128)} %bitcast.12, f32[128,512]{1,0:T(8,128)} %bitcast.13, f32[256,256]{1,0:T(8,128)} %get-tuple-element.34.a_ref, ...), custom_call_target="tpu_custom_call" | custom-call | tf_op jit(solution)/shard_map/finish/pallas_call | solution.py:265
  (52 shorter events, 4.3 us)
Async XLA Ops:
  0.0 5.2 %copy-start.2 = (f32[64,256]{1,0:T(8,128)S(1)}, f32[64,256]{1,0:T(8,128)}, u32[]{:S(2)}) copy-start(f32[64,256]{1,0:T(8,128)} %refs_4_.1) | copy-start | bytes 196612
  4.6 5.7 %collective-permute-start = (f32[128,512]{1,0:T(8,128)}, f32[128,512]{1,0:T(8,128)S(1)}, u32[]{:S(2)}, u32[]{:S(2)}) collective-permute-start(f32[128,512]{1,0:T(8,128)} %get-tuple-element.23.send), channel_id=1, source_target_pairs={{0,4},{4,0},{8,12},{12,8},{16,20},{20,16},{24,28},{28,24},{1,5},{5... | collective-permute-start | bytes 786440 | tf_op jit(solution)/shard_map/ppermute | solution.py:19
  5.2 12.1 %collective-permute-start.8 = (f32[64,256]{1,0:T(8,128)S(1)}, f32[64,256]{1,0:T(8,128)S(1)}, u32[]{:S(2)}, u32[]{:S(2)}) collective-permute-start(f32[64,256]{1,0:T(8,128)S(1)} %copy-done.2), channel_id=1, source_target_pairs={{0,16},{4,20},{8,24},{12,28},{16,0},{20,4},{24,8},{28,12},{1,17},{... | collective-permute-start | bytes 196616 | tf_op jit(solution)/shard_map/ppermute | solution.py:19
  12.9 5.2 %collective-permute-start.1 = (f32[32,512]{1,0:T(8,128)}, f32[32,512]{1,0:T(8,128)S(1)}, u32[]{:S(2)}, u32[]{:S(2)}) collective-permute-start(f32[32,512]{1,0:T(8,128)} %get-tuple-element.25), channel_id=1, source_target_pairs={{0,8},{4,12},{8,0},{12,4},{16,24},{20,28},{24,16},{28,20},{1,9},{5... | collective-permute-start | bytes 196616 | tf_op jit(solution)/shard_map/ppermute | solution.py:19
  14.5 8.1 %collective-permute-start.2 = (f32[32,512]{1,0:T(8,128)}, f32[32,512]{1,0:T(8,128)S(1)}, u32[]{:S(2)}, u32[]{:S(2)}) collective-permute-start(f32[32,512]{1,0:T(8,128)} %get-tuple-element.26), channel_id=1, source_target_pairs={{0,16},{4,20},{8,24},{12,28},{16,0},{20,4},{24,8},{28,12},{1,17},{... | collective-permute-start | bytes 196616 | tf_op jit(solution)/shard_map/ppermute | solution.py:19
  14.8 7.7 %collective-permute-start.3 = (f32[32,512]{1,0:T(8,128)}, f32[32,512]{1,0:T(8,128)S(1)}, u32[]{:S(2)}, u32[]{:S(2)}) collective-permute-start(f32[32,512]{1,0:T(8,128)} %get-tuple-element.27), channel_id=1, source_target_pairs={{0,24},{4,28},{8,16},{12,20},{16,8},{20,12},{24,0},{28,4},{1,25},{... | collective-permute-start | bytes 196616 | tf_op jit(solution)/shard_map/ppermute | solution.py:19
  17.3 12.1 %collective-permute-start.9 = (f32[64,256]{1,0:T(8,128)S(1)}, f32[64,256]{1,0:T(8,128)S(1)}, u32[]{:S(2)}, u32[]{:S(2)}) collective-permute-start(f32[64,256]{1,0:T(8,128)S(1)} %broadcast_select_fusion), channel_id=1, source_target_pairs={{0,8},{4,12},{8,0},{12,4},{16,24},{20,28},{24,16},{28,20},{1,9},{5... | collective-permute-start | bytes 196616 | tf_op jit(solution)/shard_map/ppermute | solution.py:19
  18.0 4.5 %copy-start.13 = (f32[32,512]{1,0:T(8,128)}, f32[32,512]{1,0:T(8,128)S(1)}, u32[]{:S(2)}) copy-start(f32[32,512]{1,0:T(8,128)S(1)} %collective-permute-done.1.refs_1_) | copy-start | bytes 196612
  25.0 6.1 %collective-permute-start.4 = (f32[32,512]{1,0:T(8,128)}, f32[32,512]{1,0:T(8,128)S(1)}, u32[]{:S(2)}, u32[]{:S(2)}) collective-permute-start(f32[32,512]{1,0:T(8,128)} %get-tuple-element.29), channel_id=1, source_target_pairs={{0,8},{4,12},{8,0},{12,4},{16,24},{20,28},{24,16},{28,20},{1,9},{5... | collective-permute-start | bytes 196616 | tf_op jit(solution)/shard_map/ppermute | solution.py:19
  26.5 7.6 %collective-permute-start.5 = (f32[32,512]{1,0:T(8,128)}, f32[32,512]{1,0:T(8,128)S(1)}, u32[]{:S(2)}, u32[]{:S(2)}) collective-permute-start(f32[32,512]{1,0:T(8,128)} %get-tuple-element.30), channel_id=1, source_target_pairs={{0,16},{4,20},{8,24},{12,28},{16,0},{20,4},{24,8},{28,12},{1,17},{... | collective-permute-start | bytes 196616 | tf_op jit(solution)/shard_map/ppermute | solution.py:19
  27.1 9.5 %collective-permute-start.6 = (f32[32,512]{1,0:T(8,128)}, f32[32,512]{1,0:T(8,128)S(1)}, u32[]{:S(2)}, u32[]{:S(2)}) collective-permute-start(f32[32,512]{1,0:T(8,128)} %get-tuple-element.31), channel_id=1, source_target_pairs={{0,24},{4,28},{8,16},{12,20},{16,8},{20,12},{24,0},{28,4},{1,25},{... | collective-permute-start | bytes 196616 | tf_op jit(solution)/shard_map/ppermute | solution.py:19
  29.4 9.9 %collective-permute-start.10 = (f32[64,256]{1,0:T(8,128)S(1)}, f32[64,256]{1,0:T(8,128)S(1)}, u32[]{:S(2)}, u32[]{:S(2)}) collective-permute-start(f32[64,256]{1,0:T(8,128)S(1)} %broadcast_select_fusion.1), channel_id=1, source_target_pairs={{0,4},{4,0},{8,12},{12,8},{16,20},{20,16},{24,28},{28,24},{1,5},{5... | collective-permute-start | bytes 196616 | tf_op jit(solution)/shard_map/ppermute | solution.py:19
  29.5 10.4 %collective-permute-start.15 = (f32[64,256]{1,0:T(8,128)S(1)}, f32[64,256]{1,0:T(8,128)S(1)}, u32[]{:S(2)}, u32[]{:S(2)}) collective-permute-start(f32[64,256]{1,0:T(8,128)S(1)} %copy-done.2), channel_id=1, source_target_pairs={{0,2},{1,3},{2,0},{3,1},{4,6},{5,7},{6,4},{7,5},{8,10},{9,11},{10,... | collective-permute-start | bytes 196616 | tf_op jit(solution)/shard_map/ppermute | solution.py:19
  31.0 5.6 %copy-start.4 = (f32[32,512]{1,0:T(8,128)}, f32[32,512]{1,0:T(8,128)S(1)}, u32[]{:S(2)}) copy-start(f32[32,512]{1,0:T(8,128)S(1)} %collective-permute-done.4.refs_1_) | copy-start | bytes 196612
  31.0 10.4 %collective-permute-start.14 = (f32[64,256]{1,0:T(8,128)S(1)}, f32[64,256]{1,0:T(8,128)S(1)}, u32[]{:S(2)}, u32[]{:S(2)}) collective-permute-start(f32[64,256]{1,0:T(8,128)S(1)} %copy-done.2), channel_id=1, source_target_pairs={{0,1},{1,0},{2,3},{3,2},{4,5},{5,4},{6,7},{7,6},{8,9},{9,8},{10,11... | collective-permute-start | bytes 196616 | tf_op jit(solution)/shard_map/ppermute | solution.py:19
  34.2 8.8 %collective-permute-start.16 = (f32[64,256]{1,0:T(8,128)S(1)}, f32[64,256]{1,0:T(8,128)S(1)}, u32[]{:S(2)}, u32[]{:S(2)}) collective-permute-start(f32[64,256]{1,0:T(8,128)S(1)} %copy-done.2), channel_id=1, source_target_pairs={{0,3},{1,2},{2,1},{3,0},{4,7},{5,6},{6,5},{7,4},{8,11},{9,10},{10,... | collective-permute-start | bytes 196616 | tf_op jit(solution)/shard_map/ppermute | solution.py:19
  39.3 17.4 %collective-permute-start.7 = (f32[4,32,512]{2,1,0:T(8,128)}, f32[4,32,512]{2,1,0:T(8,128)S(1)}, u32[]{:S(2)}, u32[]{:S(2)}) collective-permute-start(f32[4,32,512]{2,1,0:T(8,128)} %get-tuple-element.33), channel_id=1, source_target_pairs={{0,4},{4,0},{8,12},{12,8},{16,20},{20,16},{24,28},{28,24},{1,5},{5... | collective-permute-start | bytes 786440 | tf_op jit(solution)/shard_map/ppermute | solution.py:19
  39.3 6.4 %copy-start.3 = (f32[64,256]{1,0:T(8,128)}, f32[64,256]{1,0:T(8,128)S(1)}, u32[]{:S(2)}) copy-start(f32[64,256]{1,0:T(8,128)S(1)} %broadcast_select_fusion.2.refs_0_) | copy-start | bytes 196612
  39.4 5.9 %collective-permute-start.13 = (f32[64,256]{1,0:T(8,128)S(1)}, f32[64,256]{1,0:T(8,128)S(1)}, u32[]{:S(2)}, u32[]{:S(2)}) collective-permute-start(f32[64,256]{1,0:T(8,128)S(1)} %broadcast_select_fusion.2.refs_0_), channel_id=1, source_target_pairs={{0,3},{1,2},{2,1},{3,0},{4,7},{5,6},{6,5},{7,4},{8,11},{9,10},{10,... | collective-permute-start | bytes 196616 | tf_op jit(solution)/shard_map/ppermute | solution.py:19
  39.9 5.8 %copy-start.7 = (f32[64,256]{1,0:T(8,128)}, f32[64,256]{1,0:T(8,128)S(1)}, u32[]{:S(2)}) copy-start(f32[64,256]{1,0:T(8,128)S(1)} %collective-permute-done.15.refs_6_) | copy-start | bytes 196612
  39.9 5.6 %collective-permute-start.12 = (f32[64,256]{1,0:T(8,128)S(1)}, f32[64,256]{1,0:T(8,128)S(1)}, u32[]{:S(2)}, u32[]{:S(2)}) collective-permute-start(f32[64,256]{1,0:T(8,128)S(1)} %broadcast_select_fusion.2.refs_0_), channel_id=1, source_target_pairs={{0,2},{1,3},{2,0},{3,1},{4,6},{5,7},{6,4},{7,5},{8,10},{9,11},{10,... | collective-permute-start | bytes 196616 | tf_op jit(solution)/shard_map/ppermute | solution.py:19
  41.4 4.3 %copy-start.8 = (f32[64,256]{1,0:T(8,128)}, f32[64,256]{1,0:T(8,128)S(1)}, u32[]{:S(2)}) copy-start(f32[64,256]{1,0:T(8,128)S(1)} %collective-permute-done.14.refs_5_) | copy-start | bytes 196612
  41.4 4.3 %collective-permute-start.11 = (f32[64,256]{1,0:T(8,128)S(1)}, f32[64,256]{1,0:T(8,128)S(1)}, u32[]{:S(2)}, u32[]{:S(2)}) collective-permute-start(f32[64,256]{1,0:T(8,128)S(1)} %broadcast_select_fusion.2.refs_0_), channel_id=1, source_target_pairs={{0,1},{1,0},{2,3},{3,2},{4,5},{5,4},{6,7},{7,6},{8,9},{9,8},{10,11... | collective-permute-start | bytes 196616 | tf_op jit(solution)/shard_map/ppermute | solution.py:19
  42.9 2.8 %copy-start.9 = (f32[64,256]{1,0:T(8,128)}, f32[64,256]{1,0:T(8,128)S(1)}, u32[]{:S(2)}) copy-start(f32[64,256]{1,0:T(8,128)S(1)} %collective-permute-done.16.refs_7_) | copy-start | bytes 196612
  (9 other events, 7.6 us)
where the time goes:
time: 61.5 us; the launch traced here: 61.2 us
  Pallas kernels  25.5 us (41%)
  starting transfers between devices  22.9 us (37%)
  waiting for transfers between devices  8.92 us (15%)
  local copies, waits for them, and re-layouts  3.73 us (6%)
    ppermute x17, starting transfers between devices, pair_exchange(): return lax.ppermute(value, axis, [(i, i ^ bit) for i in range(size)])  22.9 us
    pallas_call x1, Pallas kernels, on_device(): pl.pallas_call(functools.partial(factor_body, spread), out_shape=(array(r...  9.91 us
    ppermute x17, waiting for transfers between devices, pair_exchange(): return lax.ppermute(value, axis, [(i, i ^ bit) for i in range(size)])  8.92 us
    pallas_call x1, Pallas kernels, on_device(): pl.pallas_call(pick_body, out_shape=(array(half, cols), array(half, cols)...  4.6 us
    pallas_call x1, Pallas kernels, on_device(): pl.pallas_call(functools.partial(finish_body, rows), out_shape=array(rows...  3.83 us
    unnamed x32, local copies, waits for them, and re-layouts  3.73 us
    pallas_call x1, Pallas kernels, on_device(): pl.pallas_call(functools.partial(share_body, rows), out_shape=[array(chip...  2.06 us
    pallas_call x1, Pallas kernels, on_device(): pl.pallas_call(functools.partial(chip_body, rows), out_shape=[array(size,...  1.84 us
  transfers between devices with their start and end apart: 17, of which 5 were waited for; matrix products, arithmetic and copies ran while one was open for 0% of the time, Pallas kernels for 28%

commit v1 on v0

--- a/solution.py
+++ b/solution.py
@@ -8,10 +8,10 @@
 from jax.sharding import PartitionSpec as P
 
 VMEM = pl.BlockSpec(memory_space=pltpu.VMEM)
-SMEM = pl.BlockSpec(memory_space=pltpu.SMEM)
-ANY = pl.BlockSpec(memory_space=pl.ANY)
+HBM = pl.BlockSpec(memory_space=pltpu.HBM)
 F32 = jnp.float32
 UNROLL = 32
+VMEM_LIMIT = 16 << 20
 
 
 def pair_exchange(value, axis, bit):
@@ -19,23 +19,50 @@
     return lax.ppermute(value, axis, [(i, i ^ bit) for i in range(size)])
 
 
+def call(body, outs, *args, in_specs=None, out_specs=None, scratch=()):
+    if in_specs is None:
+        in_specs = [VMEM] * len(args)
+    placed = [
+        pltpu.with_memory_space_constraint(arg, spec.memory_space)
+        for arg, spec in zip(args, in_specs)
+    ]
+    return kernel(body, outs, placed, in_specs, out_specs, scratch)
+
+
+def kernel(body, outs, placed, in_specs, out_specs, scratch):
+    return pl.pallas_call(
+        body,
+        out_shape=tuple(outs),
+        in_specs=list(in_specs),
+        out_specs=tuple(out_specs) if out_specs else (VMEM,) * len(outs),
+        scratch_shapes=list(scratch),
+        compiler_params=pltpu.CompilerParams(vmem_limit_bytes=VMEM_LIMIT),
+    )(*placed)
+
+
 def inside(rows, low, count):
     return (rows >= low) & (rows < low + count)
 
 
-def pick_body(pivots, trailing, keep, send, slots, table, block, sem):
+def pick_body(given, trailing, keep, send, column, pivots, table, slots, block, sems):
     width = pivots.shape[0]
     rows = trailing.shape[0]
+    lanes = column.shape[1]
     half = width // 2
     me = lax.axis_index("prow")
     core = lax.rem(me, 2)
     first = me * rows
-    load = pltpu.make_async_copy(trailing, block, sem)
+    order = pltpu.make_async_copy(given, pivots, sems.at[0])
+    load = pltpu.make_async_copy(trailing, block, sems.at[1])
+    order.start()
     load.start()
 
-    def fill(i, _):
+    def top(i, _):
         for u in range(UNROLL):
             table[i * UNROLL + u] = i * UNROLL + u
+        return 0
+
+    def fill(i, _):
         for u in range(UNROLL):
             pivot = pivots[i * UNROLL + u]
             table[pivot] = pivot
@@ -50,6 +77,8 @@
             table[pivot] = mine
         return 0
 
+    lax.fori_loop(0, width // UNROLL, top, 0)
+    order.wait()
     lax.fori_loop(0, width // UNROLL, fill, 0)
     lax.fori_loop(0, width // UNROLL, exchange, 0)
     load.wait()
@@ -63,6 +92,7 @@
                 own = (local >= 0) & (local < rows)
                 index = jnp.where(own, local, jnp.where(me == 0, table[row], 0))
                 target[pl.ds(j, 1), :] = block[pl.ds(index, 1), :]
+                column[pl.ds(offset + j, 1), :] = jnp.full((1, lanes), row, jnp.int32)
             return 0
 
         lax.fori_loop(0, half // UNROLL, some, 0)
@@ -71,14 +101,14 @@
     pick(core * half, keep)
 
 
-def column_body(slots, column):
-    def some(i, _):
-        for u in range(UNROLL):
-            j = i * UNROLL + u
-            column[pl.ds(j, 1), :] = jnp.full((1, column.shape[1]), slots[j], jnp.int32)
-        return 0
-
-    lax.fori_loop(0, column.shape[0] // UNROLL, some, 0)
+def mark_body(column, mark):
+    mark[...] = column[0 : mark.shape[0], :]
+
+
+def join_body(mark, panel, diag, arrived, joined):
+    del mark
+    joined[0] = jnp.where(lax.rem(lax.axis_index("prow"), 2) == 1, arrived[...], diag[...])
+    joined[1] = panel[...]
 
 
 def chip_body(rows, keep, recv, column, *pieces):
@@ -127,18 +157,19 @@
     return lax.dot(a, b, precision=lax.Precision.HIGHEST, preferred_element_type=F32)
 
 
-def factor_body(count, column, trailing, *refs):
-    diag, lower = refs[:count], refs[count : 2 * count]
-    a_ref, sel_ref, base_ref, diag_t, lower_t = refs[2 * count :]
-    depth = diag[0].shape[0]
+def factor_body(count, mark, column, trailing, *refs):
+    del mark
+    panels = refs[:count]
+    a_ref, sel_ref, base_ref, diag_t, lower_t = refs[count:]
+    depth = panels[0].shape[1]
     width = depth * count
     rows = trailing.shape[0]
     me = lax.axis_index("prow")
     mine = lax.axis_index("pcol")
     for d in range(count):
         at = pl.ds(pl.multiple_of(lax.bitwise_xor(mine, d) * depth, depth), depth)
-        diag_t[at, :] = diag[d][...]
-        lower_t[at, :] = lower[d][...]
+        diag_t[at, :] = panels[d][0]
+        lower_t[at, :] = panels[d][1]
     i = lax.broadcasted_iota(jnp.int32, (width, width), 0)
     j = lax.broadcasted_iota(jnp.int32, (width, width), 1)
     full = diag_t[...]
@@ -196,84 +227,76 @@
     assert rows == width and size * chips == half and depth * spread == width
 
     def array(*shape, dtype=F32):
-        return jax.ShapeDtypeStruct(shape, dtype)
-
-    me = lax.axis_index("prow")
-    diag = panel_t
-    bit = devices // 2
+        return pltpu.VMEM(shape, dtype)
+
+    keep, send, column = call(
+        pick_body,
+        (array(half, cols), array(half, cols), array(width, 128, dtype=jnp.int32)),
+        pivots,
+        trailing_in,
+        in_specs=(HBM, HBM),
+        scratch=(
+            pltpu.SMEM((width,), jnp.int32),
+            pltpu.SMEM((rows * devices,), jnp.int32),
+            pltpu.SMEM((width,), jnp.int32),
+            pltpu.VMEM((rows, cols), F32),
+            pltpu.SemaphoreType.DMA((2,)),
+        ),
+    )
+    me = lax.axis_index("prow")
+    diag, arrived, bit = panel_t, panel_t, devices // 2
     while bit:
-        diag = jnp.where((me & bit) > 0, pair_exchange(diag, "prow", bit), diag)
+        arrived = pair_exchange(diag, "prow", bit)
+        if bit > 1:
+            diag = jnp.where((me & bit) > 0, arrived, diag)
         bit //= 2
-    lowers = [panel_t] + [pair_exchange(panel_t, "pcol", d) for d in range(1, spread)]
-    diags = [diag] + [pair_exchange(diag, "pcol", d) for d in range(1, spread)]
-
-    keep, send, slots = pl.pallas_call(
-        pick_body,
-        out_shape=(array(half, cols), array(half, cols), array(width, dtype=jnp.int32)),
-        in_specs=[SMEM, ANY],
-        out_specs=(VMEM, VMEM, SMEM),
-        scratch_shapes=[
-            pltpu.SMEM((rows * devices,), jnp.int32),
-            pltpu.VMEM((rows, cols), F32),
-            pltpu.SemaphoreType.DMA,
-        ],
-        name="pick",
-    )(pivots, trailing_in)
-    column = pl.pallas_call(
-        column_body,
-        out_shape=array(width, 128, dtype=jnp.int32),
-        in_specs=[SMEM],
-        out_specs=VMEM,
-        name="column",
-    )(slots)
+    (mark,) = call(mark_body, (array(8, 128, dtype=jnp.int32),), column)
+    (joined,) = call(join_body, (array(2, depth, rows),), mark, panel_t, diag, arrived)
+    panels = [joined] + [pair_exchange(joined, "pcol", d) for d in range(1, spread)]
+
     recv = pair_exchange(send, "prow", 1).reshape(chips, size, cols)
     cut = keep.reshape(chips, size, cols)
     ids = column.reshape(devices, size, 128)
-    pieces = pl.pallas_call(
-        functools.partial(chip_body, rows),
-        out_shape=[array(size, cols)] * chips,
-        in_specs=[VMEM] * 3,
-        out_specs=[VMEM] * chips,
-        name="chip",
-    )(cut, recv, ids)
+    pieces = call(functools.partial(chip_body, rows), [array(size, cols)] * chips, cut, recv, ids)
     gathered = [pieces[0]] + [pair_exchange(pieces[d], "prow", 2 * d) for d in range(1, chips)]
-    parts = pl.pallas_call(
-        functools.partial(owner_body, rows, chips),
-        out_shape=[array(size, cols)] * chips,
-        in_specs=[VMEM] * (1 + chips),
-        out_specs=[VMEM] * chips,
-        name="owner",
-    )(ids, *gathered)
+    parts = call(
+        functools.partial(owner_body, rows, chips), [array(size, cols)] * chips, ids, *gathered
+    )
     parts = [parts[0]] + [pair_exchange(parts[d], "prow", 2 * d) for d in range(1, chips)]
-    own, other = pl.pallas_call(
-        functools.partial(share_body, rows),
-        out_shape=[array(chips, size, cols)] * 2,
-        in_specs=[VMEM] * (3 + chips),
-        out_specs=[VMEM] * 2,
-        name="share",
-    )(cut, recv, ids, *parts)
+    own, other = call(
+        functools.partial(share_body, rows), [array(chips, size, cols)] * 2, cut, recv, ids, *parts
+    )
     own = own.reshape(half, cols)
     arrived = pair_exchange(other, "prow", 1).reshape(half, cols)
-    a, sel, base = pl.pallas_call(
+    (mark,) = call(mark_body, (array(8, 128, dtype=jnp.int32),), column)
+    a, sel, base = call(
         functools.partial(factor_body, spread),
-        out_shape=(array(rows, width), array(rows, width, dtype=jnp.bfloat16), array(rows, cols)),
-        in_specs=[VMEM] * (2 + 2 * spread),
-        out_specs=(VMEM,) * 3,
-        scratch_shapes=[pltpu.VMEM((width, width), F32), pltpu.VMEM((width, rows), F32)],
-        name="factor",
-    )(column, trailing_in, *diags, *lowers)
-    return pl.pallas_call(
+        (array(rows, width), array(rows, width, dtype=jnp.bfloat16), array(rows, cols)),
+        mark,
+        column,
+        trailing_in,
+        *panels,
+        scratch=(pltpu.VMEM((width, width), F32), pltpu.VMEM((width, rows), F32)),
+    )
+    (out,) = call(
         functools.partial(finish_body, rows),
-        out_shape=array(rows, cols),
-        in_specs=[VMEM] * 8,
-        out_specs=VMEM,
-        name="finish",
-    )(column, keep, send, own, arrived, a, sel, base)
+        (jax.ShapeDtypeStruct((rows, cols), F32),),
+        column,
+        keep,
+        send,
+        own,
+        arrived,
+        a,
+        sel,
+        base,
+    )
+    return out
 
 
 def solution(mesh):
     in_specs = (P("prow", "pcol"), P("pcol", "prow"), P())
     out_specs = P("prow", "pcol")
+
     return jax.shard_map(
         on_device, mesh=mesh, in_specs=in_specs, out_specs=out_specs, check_vma=False
     )

time: 61.5 us -> 49.7 us (0.81)
  Pallas kernels: 25.5 us -> 14.1 us
  waiting for transfers between devices: 8.92 us -> 17.5 us
  starting transfers between devices: 22.9 us -> 17.8 us
  local copies, waits for them, and re-layouts: 3.73 us -> 0.01 us
    pallas_call x7 -> x8, Pallas kernels: 25.5 us -> 14.1 us  [kernel(): pl.pallas_call(body, out_shape=tuple(outs), in_specs=list(in_specs), out_...]
    ppermute x17 -> x14, waiting for transfers between devices: 8.92 us -> 17.5 us  [pair_exchange(): return lax.ppermute(value, axis, [(i, i ^ bit) for i in range(size)])]
    ppermute x17 -> x14, starting transfers between devices: 22.9 us -> 17.8 us  [pair_exchange(): return lax.ppermute(value, axis, [(i, i ^ bit) for i in range(size)])]
    unnamed x32 -> x4, local copies, waits for them, and re-layouts: 3.73 us -> 0.01 us
  transfers between devices with their start and end apart: 17 -> 14, of which waited for: 5 -> 7; matrix products, arithmetic and copies ran while one was open for 0% -> 0% of each run, Pallas kernels for 28% -> 16%
where the time goes in v1:
time: 49.7 us; the launch traced here: 49.5 us
  starting transfers between devices  17.8 us (36%)
  waiting for transfers between devices  17.5 us (35%)
  Pallas kernels  14.1 us (28%)
    ppermute x14, starting transfers between devices, pair_exchange(): return lax.ppermute(value, axis, [(i, i ^ bit) for i in range(size)])  17.8 us
    ppermute x14, waiting for transfers between devices, pair_exchange(): return lax.ppermute(value, axis, [(i, i ^ bit) for i in range(size)])  17.5 us
    pallas_call x8, Pallas kernels, kernel(): pl.pallas_call(body, out_shape=tuple(outs), in_specs=list(in_specs), out_...  14.1 us
  transfers between devices with their start and end apart: 14, of which 7 were waited for; matrix products, arithmetic and copies ran while one was open for 0% of the time, Pallas kernels for 16%

profile of v1, /device:TPU:0, one launch (start us, length us, event | category | flops | bytes accessed | tf_op | source)
XLA Modules:
  0.0 49.5 jit_solution(12250908110789349463)
XLA Ops:
  0.0 3.5 %shard_map.37 = (f32[128,512]{1,0:T(8,128)S(1)}, f32[128,512]{1,0:T(8,128)S(1)}, s32[256,128]{1,0:T(8,128)S(1)}) custom-call(s32[256]{0:T(256)} %given.1, f32[256,512]{1,0:T(8,128)} %trailing.3), custom_call_target="tpu_custom_call" | custom-call | tf_op jit(solution)/shard_map/pallas_call | solution.py:33
  3.5 0.6 %collective-permute-start = (f32[128,512]{1,0:T(8,128)S(1)}, f32[128,512]{1,0:T(8,128)S(1)}, u32[]{:S(2)}, u32[]{:S(2)}) collective-permute-start(f32[128,512]{1,0:T(8,128)S(1)} %get-tuple-element.23.send), channel_id=1, source_target_pairs={{0,4},{4,0},{8,12},{12,8},{16,20},{20,16},{24,28},{28,24},{1,5},{5... | collective-permute-start | bytes 786440 | tf_op jit(solution)/shard_map/ppermute | solution.py:19
  4.1 1.2 %collective-permute-done = f32[128,512]{1,0:T(8,128)S(1)} collective-permute-done((f32[128,512]{1,0:T(8,128)S(1)}, f32[128,512]{1,0:T(8,128)S(1)}, u32[]{:S(2)}, u32[]{:S(2)}) %collective-permute-start) | collective-permute-done | bytes 262176 | tf_op jit(solution)/shard_map/ppermute | solution.py:19
  5.4 3.0 %collective-permute-start.1 = (f32[32,512]{1,0:T(8,128)S(1)}, f32[32,512]{1,0:T(8,128)S(1)}, u32[]{:S(2)}, u32[]{:S(2)}) collective-permute-start(f32[32,512]{1,0:T(8,128)S(1)} %get-tuple-element.25), channel_id=1, source_target_pairs={{0,8},{4,12},{8,0},{12,4},{16,24},{20,28},{24,16},{28,20},{1,9},{5... | collective-permute-start | bytes 196616 | tf_op jit(solution)/shard_map/ppermute | solution.py:19
  8.4 2.6 %collective-permute-start.2 = (f32[32,512]{1,0:T(8,128)S(1)}, f32[32,512]{1,0:T(8,128)S(1)}, u32[]{:S(2)}, u32[]{:S(2)}) collective-permute-start(f32[32,512]{1,0:T(8,128)S(1)} %get-tuple-element.26), channel_id=1, source_target_pairs={{0,16},{4,20},{8,24},{12,28},{16,0},{20,4},{24,8},{28,12},{1,17},{... | collective-permute-start | bytes 196616 | tf_op jit(solution)/shard_map/ppermute | solution.py:19
  11.0 1.9 %collective-permute-start.8 = (f32[64,256]{1,0:T(8,128)S(1)}, f32[64,256]{1,0:T(8,128)S(1)}, u32[]{:S(2)}, u32[]{:S(2)}) collective-permute-start(f32[64,256]{1,0:T(8,128)S(1)} %copy-done.1), channel_id=1, source_target_pairs={{0,16},{4,20},{8,24},{12,28},{16,0},{20,4},{24,8},{28,12},{1,17},{... | collective-permute-start | bytes 196616 | tf_op jit(solution)/shard_map/ppermute | solution.py:19
  12.9 5.1 %collective-permute-done.2.refs_2_ = f32[32,512]{1,0:T(8,128)S(1)} collective-permute-done((f32[32,512]{1,0:T(8,128)S(1)}, f32[32,512]{1,0:T(8,128)S(1)}, u32[]{:S(2)}, u32[]{:S(2)}) %collective-permute-start.2) | collective-permute-done | bytes 65568 | tf_op jit(solution)/shard_map/ppermute | solution.py:19
  18.0 0.1 shard_map.39
  18.1 2.0 %collective-permute-start.4 = (f32[32,512]{1,0:T(8,128)S(1)}, f32[32,512]{1,0:T(8,128)S(1)}, u32[]{:S(2)}, u32[]{:S(2)}) collective-permute-start(f32[32,512]{1,0:T(8,128)S(1)} %get-tuple-element.29), channel_id=1, source_target_pairs={{0,8},{4,12},{8,0},{12,4},{16,24},{20,28},{24,16},{28,20},{1,9},{5... | collective-permute-start | bytes 196616 | tf_op jit(solution)/shard_map/ppermute | solution.py:19
  20.1 1.5 %collective-permute-start.5 = (f32[32,512]{1,0:T(8,128)S(1)}, f32[32,512]{1,0:T(8,128)S(1)}, u32[]{:S(2)}, u32[]{:S(2)}) collective-permute-start(f32[32,512]{1,0:T(8,128)S(1)} %get-tuple-element.30), channel_id=1, source_target_pairs={{0,16},{4,20},{8,24},{12,28},{16,0},{20,4},{24,8},{28,12},{1,17},{... | collective-permute-start | bytes 196616 | tf_op jit(solution)/shard_map/ppermute | solution.py:19
  21.6 1.0 %collective-permute-start.6 = (f32[32,512]{1,0:T(8,128)S(1)}, f32[32,512]{1,0:T(8,128)S(1)}, u32[]{:S(2)}, u32[]{:S(2)}) collective-permute-start(f32[32,512]{1,0:T(8,128)S(1)} %get-tuple-element.31), channel_id=1, source_target_pairs={{0,24},{4,28},{8,16},{12,20},{16,8},{20,12},{24,0},{28,4},{1,25},{... | collective-permute-start | bytes 196616 | tf_op jit(solution)/shard_map/ppermute | solution.py:19
  22.7 1.0 %collective-permute-start.9 = (f32[64,256]{1,0:T(8,128)S(1)}, f32[64,256]{1,0:T(8,128)S(1)}, u32[]{:S(2)}, u32[]{:S(2)}) collective-permute-start(f32[64,256]{1,0:T(8,128)S(1)} %broadcast_select_fusion), channel_id=1, source_target_pairs={{0,8},{4,12},{8,0},{12,4},{16,24},{20,28},{24,16},{28,20},{1,9},{5... | collective-permute-start | bytes 196616 | tf_op jit(solution)/shard_map/ppermute | solution.py:19
  23.7 1.8 %collective-permute-done.5.refs_2_ = f32[32,512]{1,0:T(8,128)S(1)} collective-permute-done((f32[32,512]{1,0:T(8,128)S(1)}, f32[32,512]{1,0:T(8,128)S(1)}, u32[]{:S(2)}, u32[]{:S(2)}) %collective-permute-start.5) | collective-permute-done | bytes 65568 | tf_op jit(solution)/shard_map/ppermute | solution.py:19
  25.6 2.2 %collective-permute-done.6.refs_3_ = f32[32,512]{1,0:T(8,128)S(1)} collective-permute-done((f32[32,512]{1,0:T(8,128)S(1)}, f32[32,512]{1,0:T(8,128)S(1)}, u32[]{:S(2)}, u32[]{:S(2)}) %collective-permute-start.6) | collective-permute-done | bytes 65568 | tf_op jit(solution)/shard_map/ppermute | solution.py:19
  27.7 0.1 shard_map.40
  28.0 0.5 %collective-permute-start.10 = (f32[64,256]{1,0:T(8,128)S(1)}, f32[64,256]{1,0:T(8,128)S(1)}, u32[]{:S(2)}, u32[]{:S(2)}) collective-permute-start(f32[64,256]{1,0:T(8,128)S(1)} %broadcast_select_fusion.1.diag), channel_id=1, source_target_pairs={{0,4},{4,0},{8,12},{12,8},{16,20},{20,16},{24,28},{28,24},{1,5},{5... | collective-permute-start | bytes 196616 | tf_op jit(solution)/shard_map/ppermute | solution.py:19
  28.5 1.0 %collective-permute-done.10.arrived = f32[64,256]{1,0:T(8,128)S(1)} collective-permute-done((f32[64,256]{1,0:T(8,128)S(1)}, f32[64,256]{1,0:T(8,128)S(1)}, u32[]{:S(2)}, u32[]{:S(2)}) %collective-permute-start.10) | collective-permute-done | bytes 65568 | tf_op jit(solution)/shard_map/ppermute | solution.py:19
  29.6 1.6 %collective-permute-start.11 = (f32[2,64,256]{2,1,0:T(8,128)S(1)}, f32[2,64,256]{2,1,0:T(8,128)S(1)}, u32[]{:S(2)}, u32[]{:S(2)}) collective-permute-start(f32[2,64,256]{2,1,0:T(8,128)S(1)} %shard_map.42.refs_0_), channel_id=1, source_target_pairs={{0,1},{1,0},{2,3},{3,2},{4,5},{5,4},{6,7},{7,6},{8,9},{9,8},{10,11... | collective-permute-start | bytes 393224 | tf_op jit(solution)/shard_map/ppermute | solution.py:19
  31.1 1.5 %collective-permute-start.12 = (f32[2,64,256]{2,1,0:T(8,128)S(1)}, f32[2,64,256]{2,1,0:T(8,128)S(1)}, u32[]{:S(2)}, u32[]{:S(2)}) collective-permute-start(f32[2,64,256]{2,1,0:T(8,128)S(1)} %shard_map.42.refs_0_), channel_id=1, source_target_pairs={{0,2},{1,3},{2,0},{3,1},{4,6},{5,7},{6,4},{7,5},{8,10},{9,11},{10,... | collective-permute-start | bytes 393224 | tf_op jit(solution)/shard_map/ppermute | solution.py:19
  32.7 0.5 collective-permute-start.13
  33.1 2.5 %collective-permute-done.11.refs_1_ = f32[2,64,256]{2,1,0:T(8,128)S(1)} collective-permute-done((f32[2,64,256]{2,1,0:T(8,128)S(1)}, f32[2,64,256]{2,1,0:T(8,128)S(1)}, u32[]{:S(2)}, u32[]{:S(2)}) %collective-permute-start.11) | collective-permute-done | bytes 131104 | tf_op jit(solution)/shard_map/ppermute | solution.py:19
  35.7 3.6 %collective-permute-done.12.refs_2_ = f32[2,64,256]{2,1,0:T(8,128)S(1)} collective-permute-done((f32[2,64,256]{2,1,0:T(8,128)S(1)}, f32[2,64,256]{2,1,0:T(8,128)S(1)}, u32[]{:S(2)}, u32[]{:S(2)}) %collective-permute-start.12) | collective-permute-done | bytes 131104 | tf_op jit(solution)/shard_map/ppermute | solution.py:19
  39.3 7.9 %shard_map.43 = (f32[256,256]{1,0:T(8,128)S(1)}, bf16[256,256]{1,0:T(8,128)(2,1)S(1)}, f32[256,512]{1,0:T(8,128)S(1)}) custom-call(s32[8,128]{1,0:T(8,128)S(1)} %shard_map.41.mark, s32[256,128]{1,0:T(8,128)S(1)} %get-tuple-element.21.column, f32[256,512]{1,0:T(8,128)S(1)} %copy-done, f32[2,64,256]{2,1,0:T(8,128)S(1)} %shard_map.42.refs_0_, ...), custom_call_target="tpu_custom_call" | custom-call | tf_op jit(solution)/shard_map/pallas_call | solution.py:33
  47.2 2.3 %shard_map.44 = f32[256,512]{1,0:T(8,128)} custom-call(s32[256,128]{1,0:T(8,128)S(1)} %get-tuple-element.21.column, f32[128,512]{1,0:T(8,128)S(1)} %get-tuple-element.22.keep, f32[128,512]{1,0:T(8,128)S(1)} %get-tuple-element.23.send, f32[128,512]{1,0:T(8,128)S(1)} %bitcast.12, f32[128,512]{1,0:T(8,128)S(1)} %bitcast.13, ...), custom_call_target="tpu_custom_call" | custom-call | tf_op jit(solution)/shard_map/pallas_call | solution.py:33
  (18 shorter events, 0.2 us)
Async XLA Ops:
  3.5 1.7 %collective-permute-start = (f32[128,512]{1,0:T(8,128)S(1)}, f32[128,512]{1,0:T(8,128)S(1)}, u32[]{:S(2)}, u32[]{:S(2)}) collective-permute-start(f32[128,512]{1,0:T(8,128)S(1)} %get-tuple-element.23.send), channel_id=1, source_target_pairs={{0,4},{4,0},{8,12},{12,8},{16,20},{20,16},{24,28},{28,24},{1,5},{5... | collective-permute-start | bytes 786440 | tf_op jit(solution)/shard_map/ppermute | solution.py:19
  5.3 5.7 %copy-start.1 = (f32[64,256]{1,0:T(8,128)S(1)}, f32[64,256]{1,0:T(8,128)}, u32[]{:S(2)}) copy-start(f32[64,256]{1,0:T(8,128)} %panel.1) | copy-start | bytes 196612
  5.4 7.5 %collective-permute-start.1 = (f32[32,512]{1,0:T(8,128)S(1)}, f32[32,512]{1,0:T(8,128)S(1)}, u32[]{:S(2)}, u32[]{:S(2)}) collective-permute-start(f32[32,512]{1,0:T(8,128)S(1)} %get-tuple-element.25), channel_id=1, source_target_pairs={{0,8},{4,12},{8,0},{12,4},{16,24},{20,28},{24,16},{28,20},{1,9},{5... | collective-permute-start | bytes 196616 | tf_op jit(solution)/shard_map/ppermute | solution.py:19
  8.4 9.6 %collective-permute-start.2 = (f32[32,512]{1,0:T(8,128)S(1)}, f32[32,512]{1,0:T(8,128)S(1)}, u32[]{:S(2)}, u32[]{:S(2)}) collective-permute-start(f32[32,512]{1,0:T(8,128)S(1)} %get-tuple-element.26), channel_id=1, source_target_pairs={{0,16},{4,20},{8,24},{12,28},{16,0},{20,4},{24,8},{28,12},{1,17},{... | collective-permute-start | bytes 196616 | tf_op jit(solution)/shard_map/ppermute | solution.py:19
  11.0 7.0 %collective-permute-start.3 = (f32[32,512]{1,0:T(8,128)S(1)}, f32[32,512]{1,0:T(8,128)S(1)}, u32[]{:S(2)}, u32[]{:S(2)}) collective-permute-start(f32[32,512]{1,0:T(8,128)S(1)} %get-tuple-element.27), channel_id=1, source_target_pairs={{0,24},{4,28},{8,16},{12,20},{16,8},{20,12},{24,0},{28,4},{1,25},{... | collective-permute-start | bytes 196616 | tf_op jit(solution)/shard_map/ppermute | solution.py:19
  11.0 11.7 %collective-permute-start.8 = (f32[64,256]{1,0:T(8,128)S(1)}, f32[64,256]{1,0:T(8,128)S(1)}, u32[]{:S(2)}, u32[]{:S(2)}) collective-permute-start(f32[64,256]{1,0:T(8,128)S(1)} %copy-done.1), channel_id=1, source_target_pairs={{0,16},{4,20},{8,24},{12,28},{16,0},{20,4},{24,8},{28,12},{1,17},{... | collective-permute-start | bytes 196616 | tf_op jit(solution)/shard_map/ppermute | solution.py:19
  18.1 5.6 %collective-permute-start.4 = (f32[32,512]{1,0:T(8,128)S(1)}, f32[32,512]{1,0:T(8,128)S(1)}, u32[]{:S(2)}, u32[]{:S(2)}) collective-permute-start(f32[32,512]{1,0:T(8,128)S(1)} %get-tuple-element.29), channel_id=1, source_target_pairs={{0,8},{4,12},{8,0},{12,4},{16,24},{20,28},{24,16},{28,20},{1,9},{5... | collective-permute-start | bytes 196616 | tf_op jit(solution)/shard_map/ppermute | solution.py:19
  20.1 5.4 %collective-permute-start.5 = (f32[32,512]{1,0:T(8,128)S(1)}, f32[32,512]{1,0:T(8,128)S(1)}, u32[]{:S(2)}, u32[]{:S(2)}) collective-permute-start(f32[32,512]{1,0:T(8,128)S(1)} %get-tuple-element.30), channel_id=1, source_target_pairs={{0,16},{4,20},{8,24},{12,28},{16,0},{20,4},{24,8},{28,12},{1,17},{... | collective-permute-start | bytes 196616 | tf_op jit(solution)/shard_map/ppermute | solution.py:19
  21.6 6.1 %collective-permute-start.6 = (f32[32,512]{1,0:T(8,128)S(1)}, f32[32,512]{1,0:T(8,128)S(1)}, u32[]{:S(2)}, u32[]{:S(2)}) collective-permute-start(f32[32,512]{1,0:T(8,128)S(1)} %get-tuple-element.31), channel_id=1, source_target_pairs={{0,24},{4,28},{8,16},{12,20},{16,8},{20,12},{24,0},{28,4},{1,25},{... | collective-permute-start | bytes 196616 | tf_op jit(solution)/shard_map/ppermute | solution.py:19
  22.7 5.3 %collective-permute-start.9 = (f32[64,256]{1,0:T(8,128)S(1)}, f32[64,256]{1,0:T(8,128)S(1)}, u32[]{:S(2)}, u32[]{:S(2)}) collective-permute-start(f32[64,256]{1,0:T(8,128)S(1)} %broadcast_select_fusion), channel_id=1, source_target_pairs={{0,8},{4,12},{8,0},{12,4},{16,24},{20,28},{24,16},{28,20},{1,9},{5... | collective-permute-start | bytes 196616 | tf_op jit(solution)/shard_map/ppermute | solution.py:19
  27.9 11.4 %copy-start = (f32[256,512]{1,0:T(8,128)S(1)}, f32[256,512]{1,0:T(8,128)}, u32[]{:S(2)}) copy-start(f32[256,512]{1,0:T(8,128)} %trailing.3) | copy-start | bytes 1572868
  27.9 19.3 %collective-permute-start.7 = (f32[4,32,512]{2,1,0:T(8,128)S(1)}, f32[4,32,512]{2,1,0:T(8,128)S(1)}, u32[]{:S(2)}, u32[]{:S(2)}) collective-permute-start(f32[4,32,512]{2,1,0:T(8,128)S(1)} %get-tuple-element.33), channel_id=1, source_target_pairs={{0,4},{4,0},{8,12},{12,8},{16,20},{20,16},{24,28},{28,24},{1,5},{5... | collective-permute-start | bytes 786440 | tf_op jit(solution)/shard_map/ppermute | solution.py:19
  28.0 1.6 %collective-permute-start.10 = (f32[64,256]{1,0:T(8,128)S(1)}, f32[64,256]{1,0:T(8,128)S(1)}, u32[]{:S(2)}, u32[]{:S(2)}) collective-permute-start(f32[64,256]{1,0:T(8,128)S(1)} %broadcast_select_fusion.1.diag), channel_id=1, source_target_pairs={{0,4},{4,0},{8,12},{12,8},{16,20},{20,16},{24,28},{28,24},{1,5},{5... | collective-permute-start | bytes 196616 | tf_op jit(solution)/shard_map/ppermute | solution.py:19
  29.6 6.1 %collective-permute-start.11 = (f32[2,64,256]{2,1,0:T(8,128)S(1)}, f32[2,64,256]{2,1,0:T(8,128)S(1)}, u32[]{:S(2)}, u32[]{:S(2)}) collective-permute-start(f32[2,64,256]{2,1,0:T(8,128)S(1)} %shard_map.42.refs_0_), channel_id=1, source_target_pairs={{0,1},{1,0},{2,3},{3,2},{4,5},{5,4},{6,7},{7,6},{8,9},{9,8},{10,11... | collective-permute-start | bytes 393224 | tf_op jit(solution)/shard_map/ppermute | solution.py:19
  31.1 8.1 %collective-permute-start.12 = (f32[2,64,256]{2,1,0:T(8,128)S(1)}, f32[2,64,256]{2,1,0:T(8,128)S(1)}, u32[]{:S(2)}, u32[]{:S(2)}) collective-permute-start(f32[2,64,256]{2,1,0:T(8,128)S(1)} %shard_map.42.refs_0_), channel_id=1, source_target_pairs={{0,2},{1,3},{2,0},{3,1},{4,6},{5,7},{6,4},{7,5},{8,10},{9,11},{10,... | collective-permute-start | bytes 393224 | tf_op jit(solution)/shard_map/ppermute | solution.py:19
  32.7 6.6 %collective-permute-start.13 = (f32[2,64,256]{2,1,0:T(8,128)S(1)}, f32[2,64,256]{2,1,0:T(8,128)S(1)}, u32[]{:S(2)}, u32[]{:S(2)}) collective-permute-start(f32[2,64,256]{2,1,0:T(8,128)S(1)} %shard_map.42.refs_0_), channel_id=1, source_target_pairs={{0,3},{1,2},{2,1},{3,0},{4,7},{5,6},{6,5},{7,4},{8,11},{9,10},{10,... | collective-permute-start | bytes 393224 | tf_op jit(solution)/shard_map/ppermute | solution.py:19

commit v2 on v1

--- a/solution.py
+++ b/solution.py
@@ -11,6 +11,7 @@
 HBM = pl.BlockSpec(memory_space=pltpu.HBM)
 F32 = jnp.float32
 UNROLL = 32
+OUT_PIECES = 2
 VMEM_LIMIT = 16 << 20
 
 
@@ -51,7 +52,6 @@
     half = width // 2
     me = lax.axis_index("prow")
     core = lax.rem(me, 2)
-    first = me * rows
     order = pltpu.make_async_copy(given, pivots, sems.at[0])
     load = pltpu.make_async_copy(trailing, block, sems.at[1])
     order.start()
@@ -75,6 +75,7 @@
             mine = table[k]
             slots[k] = table[pivot]
             table[pivot] = mine
+            table[k] = k
         return 0
 
     lax.fori_loop(0, width // UNROLL, top, 0)
@@ -83,22 +84,26 @@
     lax.fori_loop(0, width // UNROLL, exchange, 0)
     load.wait()
 
-    def pick(offset, target):
+    def pick(offset, target, index):
         def some(i, _):
             for u in range(UNROLL):
                 j = i * UNROLL + u
                 row = slots[offset + j]
-                local = row - first
-                own = (local >= 0) & (local < rows)
-                index = jnp.where(own, local, jnp.where(me == 0, table[row], 0))
-                target[pl.ds(j, 1), :] = block[pl.ds(index, 1), :]
+                target[pl.ds(j, 1), :] = block[pl.ds(index(row), 1), :]
                 column[pl.ds(offset + j, 1), :] = jnp.full((1, lanes), row, jnp.int32)
             return 0
 
         lax.fori_loop(0, half // UNROLL, some, 0)
 
-    pick((1 - core) * half, send)
-    pick(core * half, keep)
+    @pl.when(me == 0)
+    def _():
+        pick((1 - core) * half, send, lambda row: table[row])
+        pick(core * half, keep, lambda row: table[row])
+
+    @pl.when(me != 0)
+    def _():
+        pick((1 - core) * half, send, lambda row: row & (rows - 1))
+        pick(core * half, keep, lambda row: row & (rows - 1))
 
 
 def mark_body(column, mark):
@@ -157,6 +162,46 @@
     return lax.dot(a, b, precision=lax.Precision.HIGHEST, preferred_element_type=F32)
 
 
+def triangle(blocks):
+    width = blocks[0].shape[0]
+    i = lax.broadcasted_iota(jnp.int32, (width, width), 0)
+    j = lax.broadcasted_iota(jnp.int32, (width, width), 1)
+    inverses = [(i == j).astype(F32)] * len(blocks)
+    size = 1
+    while size < width:
+        span = min(4 * size, width)
+        cross = (i // size < j // size) & (i // span == j // span)
+        steps = [jnp.where(cross, block, 0.0) for block in blocks]
+        if size > 1:
+            steps = [dot(inverse, step) for inverse, step in zip(inverses, steps)]
+        once = [
+            inverse - (step if size == 1 else dot(step, inverse))
+            for inverse, step in zip(inverses, steps)
+        ]
+        if span > 2 * size:
+            twice = [dot(step, step) for step in steps]
+            once = [part + dot(square, part) for square, part in zip(twice, once)]
+        inverses = once
+        size = span
+    return inverses
+
+
+def solve_upper(full, right):
+    width = full.shape[0]
+    half, part = width // 2, width // 4
+    cuts = [slice(k * part, (k + 1) * part) for k in range(4)]
+    small = triangle([full[cut, cut] for cut in cuts])
+    large = []
+    for k in (0, 2):
+        corner = -dot(small[k], dot(full[cuts[k], cuts[k + 1]], small[k + 1]))
+        upper = jnp.concatenate([small[k], corner], axis=1)
+        lower = jnp.concatenate([jnp.zeros_like(corner), small[k + 1]], axis=1)
+        large.append(jnp.concatenate([upper, lower], axis=0))
+    second = dot(large[1], right[half:])
+    first = dot(large[0], right[:half] - dot(full[:half, half:], second))
+    return jnp.concatenate([first, second], axis=0)
+
+
 def factor_body(count, mark, column, trailing, *refs):
     del mark
     panels = refs[:count]
@@ -170,18 +215,10 @@
         at = pl.ds(pl.multiple_of(lax.bitwise_xor(mine, d) * depth, depth), depth)
         diag_t[at, :] = panels[d][0]
         lower_t[at, :] = panels[d][1]
-    i = lax.broadcasted_iota(jnp.int32, (width, width), 0)
-    j = lax.broadcasted_iota(jnp.int32, (width, width), 1)
-    full = diag_t[...]
-    inverse = (i == j).astype(F32)
-    size = 1
-    while size < width:
-        cross = (i // size + 1 == j // size) & (lax.rem(i // size, 2) == 0)
-        block = jnp.where(cross, full, 0.0)
-        inverse = inverse - (block if size == 1 else dot(inverse, dot(block, inverse)))
-        size *= 2
-    minus = -dot(inverse, lower_t[...])
-    a_ref[...] = jnp.where(me == 0, inverse, minus).T
+    i = lax.broadcasted_iota(jnp.int32, (width, rows), 0)
+    j = lax.broadcasted_iota(jnp.int32, (width, rows), 1)
+    right = jnp.where(me == 0, (i == j).astype(F32), -lower_t[...])
+    a_ref[...] = solve_upper(diag_t[...], right).T
     ids = column[...].astype(F32).T[0:1, :]
     own = (me * rows + lax.broadcasted_iota(jnp.int32, (rows, width), 0)).astype(F32)
     match = (ids == own) & (me > 0)
@@ -191,28 +228,42 @@
     base_ref[...] = jnp.where(drop, 0.0, trailing[...])
 
 
-def finish_body(rows, column, keep, send, own, recv, a_ref, sel_ref, base, out):
+def update(rows, start, column, picked, arrived, a_ref, sel_ref, at):
+    half = picked.shape[0]
+    slots = pl.ds(pl.multiple_of(start, half), half)
+    ids = column[slots, 0:1]
+    value = arrived[:, at]
+    chosen = jnp.where(inside(ids, lax.axis_index("prow") * rows, rows), picked[:, at], value)
+    high = value.astype(jnp.bfloat16)
+    rest = value - high.astype(F32)
+    middle = rest.astype(jnp.bfloat16)
+    low = (rest - middle.astype(F32)).astype(jnp.bfloat16)
+    sel = sel_ref[:, slots]
+    total = dot(a_ref[:, slots], chosen)
+    for term in (low, middle, high):
+        total += lax.dot(sel, term, preferred_element_type=F32)
+    return total
+
+
+def half_body(rows, column, keep, own, a_ref, sel_ref, base, out):
     half = keep.shape[0]
-    me = lax.axis_index("prow")
-    core = lax.rem(me, 2)
-
-    def part(start, picked, arrived):
-        at = pl.ds(pl.multiple_of(start, half), half)
-        ids = column[at, 0:1]
-        value = arrived[...]
-        chosen = jnp.where(inside(ids, me * rows, rows), picked[...], value)
-        high = value.astype(jnp.bfloat16)
-        rest = value - high.astype(F32)
-        middle = rest.astype(jnp.bfloat16)
-        low = (rest - middle.astype(F32)).astype(jnp.bfloat16)
-        sel = sel_ref[:, at]
-        total = dot(a_ref[:, at], chosen)
-        for term in (low, middle, high):
-            total += lax.dot(sel, term, preferred_element_type=F32)
-        return total
-
-    first = part(core * half, keep, own)
-    out[...] = base[...] + first + part((1 - core) * half, send, recv)
+    start = lax.rem(lax.axis_index("prow"), 2) * half
+    out[...] = base[...] + update(rows, start, column, keep, own, a_ref, sel_ref, slice(None))
+
+
+def finish_body(rows, column, send, recv, a_ref, sel_ref, partial, out, block, sems):
+    half = send.shape[0]
+    start = (1 - lax.rem(lax.axis_index("prow"), 2)) * half
+    pieces = sems.shape[0]
+    width = out.shape[1] // pieces
+    copies = []
+    for k in range(pieces):
+        at = slice(k * width, (k + 1) * width)
+        block[:, at] = partial[:, at] + update(rows, start, column, send, recv, a_ref, sel_ref, at)
+        copies.append(pltpu.make_async_copy(block.at[:, at], out.at[:, at], sems.at[k]))
+        copies[-1].start()
+    for copy in copies:
+        copy.wait()
 
 
 def on_device(trailing_in, panel_t, pivots):
@@ -224,7 +275,7 @@
     spread = lax.axis_size("pcol")
     size = half // chips
     depth = panel_t.shape[0]
-    assert rows == width and size * chips == half and depth * spread == width
+    assert rows == width and rows & (rows - 1) == 0 and size * chips == half and depth * spread == width
 
     def array(*shape, dtype=F32):
         return pltpu.VMEM(shape, dtype)
@@ -278,17 +329,20 @@
         *panels,
         scratch=(pltpu.VMEM((width, width), F32), pltpu.VMEM((width, rows), F32)),
     )
+    (partial,) = call(
+        functools.partial(half_body, rows), (array(rows, cols),), column, keep, own, a, sel, base
+    )
     (out,) = call(
         functools.partial(finish_body, rows),
         (jax.ShapeDtypeStruct((rows, cols), F32),),
         column,
-        keep,
         send,
-        own,
         arrived,
         a,
         sel,
-        base,
+        partial,
+        out_specs=(HBM,),
+        scratch=(pltpu.VMEM((rows, cols), F32), pltpu.SemaphoreType.DMA((OUT_PIECES,))),
     )
     return out
 

time: 49.7 us -> 44.6 us (0.90)
  Pallas kernels: 14.1 us -> 9.06 us
    pallas_call x8 -> x9, Pallas kernels: 14.1 us -> 9.06 us  [kernel(): pl.pallas_call(body, out_shape=tuple(outs), in_specs=list(in_specs), out_...]
  transfers between devices with their start and end apart: 14 -> 14, of which waited for: 7 -> 7; matrix products, arithmetic and copies ran while one was open for 0% -> 0% of each run, Pallas kernels for 16% -> 9%
where the time goes in v2:
time: 44.6 us; the launch traced here: 44.5 us
  starting transfers between devices  17.8 us (40%)
  waiting for transfers between devices  17.5 us (39%)
  Pallas kernels  9.06 us (20%)
    ppermute x14, starting transfers between devices, pair_exchange(): return lax.ppermute(value, axis, [(i, i ^ bit) for i in range(size)])  17.8 us
    ppermute x14, waiting for transfers between devices, pair_exchange(): return lax.ppermute(value, axis, [(i, i ^ bit) for i in range(size)])  17.5 us
    pallas_call x9, Pallas kernels, kernel(): pl.pallas_call(body, out_shape=tuple(outs), in_specs=list(in_specs), out_...  9.06 us
  transfers between devices with their start and end apart: 14, of which 7 were waited for; matrix products, arithmetic and copies ran while one was open for 0% of the time, Pallas kernels for 9%

profile of v2, /device:TPU:0, one launch (start us, length us, event | category | flops | bytes accessed | tf_op | source)
XLA Modules:
  0.0 44.5 jit_solution(11535497120024536680)
XLA Ops:
  0.0 3.2 %shard_map.37 = (f32[128,512]{1,0:T(8,128)S(1)}, f32[128,512]{1,0:T(8,128)S(1)}, s32[256,128]{1,0:T(8,128)S(1)}) custom-call(s32[256]{0:T(256)} %given.1, f32[256,512]{1,0:T(8,128)} %trailing.3), custom_call_target="tpu_custom_call" | custom-call | tf_op jit(solution)/shard_map/pallas_call | solution.py:34
  3.2 0.6 %collective-permute-start = (f32[128,512]{1,0:T(8,128)S(1)}, f32[128,512]{1,0:T(8,128)S(1)}, u32[]{:S(2)}, u32[]{:S(2)}) collective-permute-start(f32[128,512]{1,0:T(8,128)S(1)} %get-tuple-element.22.send), channel_id=1, source_target_pairs={{0,4},{4,0},{8,12},{12,8},{16,20},{20,16},{24,28},{28,24},{1,5},{5... | collective-permute-start | bytes 786440 | tf_op jit(solution)/shard_map/ppermute | solution.py:20
  3.8 1.2 %collective-permute-done = f32[128,512]{1,0:T(8,128)S(1)} collective-permute-done((f32[128,512]{1,0:T(8,128)S(1)}, f32[128,512]{1,0:T(8,128)S(1)}, u32[]{:S(2)}, u32[]{:S(2)}) %collective-permute-start) | collective-permute-done | bytes 262176 | tf_op jit(solution)/shard_map/ppermute | solution.py:20
  5.1 3.0 %collective-permute-start.1 = (f32[32,512]{1,0:T(8,128)S(1)}, f32[32,512]{1,0:T(8,128)S(1)}, u32[]{:S(2)}, u32[]{:S(2)}) collective-permute-start(f32[32,512]{1,0:T(8,128)S(1)} %get-tuple-element.25), channel_id=1, source_target_pairs={{0,8},{4,12},{8,0},{12,4},{16,24},{20,28},{24,16},{28,20},{1,9},{5... | collective-permute-start | bytes 196616 | tf_op jit(solution)/shard_map/ppermute | solution.py:20
  8.1 2.6 %collective-permute-start.2 = (f32[32,512]{1,0:T(8,128)S(1)}, f32[32,512]{1,0:T(8,128)S(1)}, u32[]{:S(2)}, u32[]{:S(2)}) collective-permute-start(f32[32,512]{1,0:T(8,128)S(1)} %get-tuple-element.26), channel_id=1, source_target_pairs={{0,16},{4,20},{8,24},{12,28},{16,0},{20,4},{24,8},{28,12},{1,17},{... | collective-permute-start | bytes 196616 | tf_op jit(solution)/shard_map/ppermute | solution.py:20
  10.7 1.9 %collective-permute-start.8 = (f32[64,256]{1,0:T(8,128)S(1)}, f32[64,256]{1,0:T(8,128)S(1)}, u32[]{:S(2)}, u32[]{:S(2)}) collective-permute-start(f32[64,256]{1,0:T(8,128)S(1)} %copy-done.1), channel_id=1, source_target_pairs={{0,16},{4,20},{8,24},{12,28},{16,0},{20,4},{24,8},{28,12},{1,17},{... | collective-permute-start | bytes 196616 | tf_op jit(solution)/shard_map/ppermute | solution.py:20
  12.6 5.1 %collective-permute-done.2.refs_2_ = f32[32,512]{1,0:T(8,128)S(1)} collective-permute-done((f32[32,512]{1,0:T(8,128)S(1)}, f32[32,512]{1,0:T(8,128)S(1)}, u32[]{:S(2)}, u32[]{:S(2)}) %collective-permute-start.2) | collective-permute-done | bytes 65568 | tf_op jit(solution)/shard_map/ppermute | solution.py:20
  17.8 2.0 %collective-permute-start.4 = (f32[32,512]{1,0:T(8,128)S(1)}, f32[32,512]{1,0:T(8,128)S(1)}, u32[]{:S(2)}, u32[]{:S(2)}) collective-permute-start(f32[32,512]{1,0:T(8,128)S(1)} %get-tuple-element.29), channel_id=1, source_target_pairs={{0,8},{4,12},{8,0},{12,4},{16,24},{20,28},{24,16},{28,20},{1,9},{5... | collective-permute-start | bytes 196616 | tf_op jit(solution)/shard_map/ppermute | solution.py:20
  19.8 1.5 %collective-permute-start.5 = (f32[32,512]{1,0:T(8,128)S(1)}, f32[32,512]{1,0:T(8,128)S(1)}, u32[]{:S(2)}, u32[]{:S(2)}) collective-permute-start(f32[32,512]{1,0:T(8,128)S(1)} %get-tuple-element.30), channel_id=1, source_target_pairs={{0,16},{4,20},{8,24},{12,28},{16,0},{20,4},{24,8},{28,12},{1,17},{... | collective-permute-start | bytes 196616 | tf_op jit(solution)/shard_map/ppermute | solution.py:20
  21.4 1.0 %collective-permute-start.6 = (f32[32,512]{1,0:T(8,128)S(1)}, f32[32,512]{1,0:T(8,128)S(1)}, u32[]{:S(2)}, u32[]{:S(2)}) collective-permute-start(f32[32,512]{1,0:T(8,128)S(1)} %get-tuple-element.31), channel_id=1, source_target_pairs={{0,24},{4,28},{8,16},{12,20},{16,8},{20,12},{24,0},{28,4},{1,25},{... | collective-permute-start | bytes 196616 | tf_op jit(solution)/shard_map/ppermute | solution.py:20
  22.4 1.0 %collective-permute-start.9 = (f32[64,256]{1,0:T(8,128)S(1)}, f32[64,256]{1,0:T(8,128)S(1)}, u32[]{:S(2)}, u32[]{:S(2)}) collective-permute-start(f32[64,256]{1,0:T(8,128)S(1)} %broadcast_select_fusion), channel_id=1, source_target_pairs={{0,8},{4,12},{8,0},{12,4},{16,24},{20,28},{24,16},{28,20},{1,9},{5... | collective-permute-start | bytes 196616 | tf_op jit(solution)/shard_map/ppermute | solution.py:20
  23.4 1.8 %collective-permute-done.5.refs_2_ = f32[32,512]{1,0:T(8,128)S(1)} collective-permute-done((f32[32,512]{1,0:T(8,128)S(1)}, f32[32,512]{1,0:T(8,128)S(1)}, u32[]{:S(2)}, u32[]{:S(2)}) %collective-permute-start.5) | collective-permute-done | bytes 65568 | tf_op jit(solution)/shard_map/ppermute | solution.py:20
  25.3 2.2 %collective-permute-done.6.refs_3_ = f32[32,512]{1,0:T(8,128)S(1)} collective-permute-done((f32[32,512]{1,0:T(8,128)S(1)}, f32[32,512]{1,0:T(8,128)S(1)}, u32[]{:S(2)}, u32[]{:S(2)}) %collective-permute-start.6) | collective-permute-done | bytes 65568 | tf_op jit(solution)/shard_map/ppermute | solution.py:20
  27.4 0.1 shard_map.40
  27.7 0.5 %collective-permute-start.10 = (f32[64,256]{1,0:T(8,128)S(1)}, f32[64,256]{1,0:T(8,128)S(1)}, u32[]{:S(2)}, u32[]{:S(2)}) collective-permute-start(f32[64,256]{1,0:T(8,128)S(1)} %broadcast_select_fusion.1.diag), channel_id=1, source_target_pairs={{0,4},{4,0},{8,12},{12,8},{16,20},{20,16},{24,28},{28,24},{1,5},{5... | collective-permute-start | bytes 196616 | tf_op jit(solution)/shard_map/ppermute | solution.py:20
  28.2 1.0 %collective-permute-done.10.arrived = f32[64,256]{1,0:T(8,128)S(1)} collective-permute-done((f32[64,256]{1,0:T(8,128)S(1)}, f32[64,256]{1,0:T(8,128)S(1)}, u32[]{:S(2)}, u32[]{:S(2)}) %collective-permute-start.10) | collective-permute-done | bytes 65568 | tf_op jit(solution)/shard_map/ppermute | solution.py:20
  29.3 1.6 %collective-permute-start.11 = (f32[2,64,256]{2,1,0:T(8,128)S(1)}, f32[2,64,256]{2,1,0:T(8,128)S(1)}, u32[]{:S(2)}, u32[]{:S(2)}) collective-permute-start(f32[2,64,256]{2,1,0:T(8,128)S(1)} %shard_map.42.refs_0_), channel_id=1, source_target_pairs={{0,1},{1,0},{2,3},{3,2},{4,5},{5,4},{6,7},{7,6},{8,9},{9,8},{10,11... | collective-permute-start | bytes 393224 | tf_op jit(solution)/shard_map/ppermute | solution.py:20
  30.8 1.5 %collective-permute-start.12 = (f32[2,64,256]{2,1,0:T(8,128)S(1)}, f32[2,64,256]{2,1,0:T(8,128)S(1)}, u32[]{:S(2)}, u32[]{:S(2)}) collective-permute-start(f32[2,64,256]{2,1,0:T(8,128)S(1)} %shard_map.42.refs_0_), channel_id=1, source_target_pairs={{0,2},{1,3},{2,0},{3,1},{4,6},{5,7},{6,4},{7,5},{8,10},{9,11},{10,... | collective-permute-start | bytes 393224 | tf_op jit(solution)/shard_map/ppermute | solution.py:20
  32.4 0.5 %collective-permute-start.13 = (f32[2,64,256]{2,1,0:T(8,128)S(1)}, f32[2,64,256]{2,1,0:T(8,128)S(1)}, u32[]{:S(2)}, u32[]{:S(2)}) collective-permute-start(f32[2,64,256]{2,1,0:T(8,128)S(1)} %shard_map.42.refs_0_), channel_id=1, source_target_pairs={{0,3},{1,2},{2,1},{3,0},{4,7},{5,6},{6,5},{7,4},{8,11},{9,10},{10,... | collective-permute-start | bytes 393224 | tf_op jit(solution)/shard_map/ppermute | solution.py:20
  32.8 2.5 %collective-permute-done.11.refs_1_ = f32[2,64,256]{2,1,0:T(8,128)S(1)} collective-permute-done((f32[2,64,256]{2,1,0:T(8,128)S(1)}, f32[2,64,256]{2,1,0:T(8,128)S(1)}, u32[]{:S(2)}, u32[]{:S(2)}) %collective-permute-start.11) | collective-permute-done | bytes 131104 | tf_op jit(solution)/shard_map/ppermute | solution.py:20
  35.4 3.6 %collective-permute-done.12.refs_2_ = f32[2,64,256]{2,1,0:T(8,128)S(1)} collective-permute-done((f32[2,64,256]{2,1,0:T(8,128)S(1)}, f32[2,64,256]{2,1,0:T(8,128)S(1)}, u32[]{:S(2)}, u32[]{:S(2)}) %collective-permute-start.12) | collective-permute-done | bytes 131104 | tf_op jit(solution)/shard_map/ppermute | solution.py:20
  39.0 3.1 %shard_map.43 = (f32[256,256]{1,0:T(8,128)S(1)}, bf16[256,256]{1,0:T(8,128)(2,1)S(1)}, f32[256,512]{1,0:T(8,128)S(1)}) custom-call(s32[8,128]{1,0:T(8,128)S(1)} %shard_map.41.mark, s32[256,128]{1,0:T(8,128)S(1)} %get-tuple-element.21.column, f32[256,512]{1,0:T(8,128)S(1)} %copy-done, f32[2,64,256]{2,1,0:T(8,128)S(1)} %shard_map.42.refs_0_, ...), custom_call_target="tpu_custom_call" | custom-call | tf_op jit(solution)/shard_map/pallas_call | solution.py:34
  42.1 0.8 %shard_map.44.partial = f32[256,512]{1,0:T(8,128)S(1)} custom-call(s32[256,128]{1,0:T(8,128)S(1)} %get-tuple-element.21.column, f32[128,512]{1,0:T(8,128)S(1)} %get-tuple-element.23.keep, f32[128,512]{1,0:T(8,128)S(1)} %bitcast.12, f32[256,256]{1,0:T(8,128)S(1)} %get-tuple-element.33.a_ref, bf16[256,256]{1,0:T(8,128)(2,1)S(1)} %get-tuple-element.34.sel_ref, ...), custom_call_target="tpu_custom_call" | custom-call | tf_op jit(solution)/shard_map/pallas_call | solution.py:34
  43.0 1.5 %shard_map.45 = f32[256,512]{1,0:T(8,128)} custom-call(s32[256,128]{1,0:T(8,128)S(1)} %get-tuple-element.21.column, f32[128,512]{1,0:T(8,128)S(1)} %get-tuple-element.22.send, f32[128,512]{1,0:T(8,128)S(1)} %bitcast.13, f32[256,256]{1,0:T(8,128)S(1)} %get-tuple-element.33.a_ref, bf16[256,256]{1,0:T(8,128)(2,1)S(1)} %get-tuple-element.34.sel_ref, ...), custom_call_target="tpu_custom_call" | custom-call | tf_op jit(solution)/shard_map/pallas_call | solution.py:34
  (19 shorter events, 0.3 us)
Async XLA Ops:
  3.2 1.7 %collective-permute-start = (f32[128,512]{1,0:T(8,128)S(1)}, f32[128,512]{1,0:T(8,128)S(1)}, u32[]{:S(2)}, u32[]{:S(2)}) collective-permute-start(f32[128,512]{1,0:T(8,128)S(1)} %get-tuple-element.22.send), channel_id=1, source_target_pairs={{0,4},{4,0},{8,12},{12,8},{16,20},{20,16},{24,28},{28,24},{1,5},{5... | collective-permute-start | bytes 786440 | tf_op jit(solution)/shard_map/ppermute | solution.py:20
  5.0 5.7 %copy-start.1 = (f32[64,256]{1,0:T(8,128)S(1)}, f32[64,256]{1,0:T(8,128)}, u32[]{:S(2)}) copy-start(f32[64,256]{1,0:T(8,128)} %panel.1) | copy-start | bytes 196612
  5.1 7.5 %collective-permute-start.1 = (f32[32,512]{1,0:T(8,128)S(1)}, f32[32,512]{1,0:T(8,128)S(1)}, u32[]{:S(2)}, u32[]{:S(2)}) collective-permute-start(f32[32,512]{1,0:T(8,128)S(1)} %get-tuple-element.25), channel_id=1, source_target_pairs={{0,8},{4,12},{8,0},{12,4},{16,24},{20,28},{24,16},{28,20},{1,9},{5... | collective-permute-start | bytes 196616 | tf_op jit(solution)/shard_map/ppermute | solution.py:20
  8.1 9.6 %collective-permute-start.2 = (f32[32,512]{1,0:T(8,128)S(1)}, f32[32,512]{1,0:T(8,128)S(1)}, u32[]{:S(2)}, u32[]{:S(2)}) collective-permute-start(f32[32,512]{1,0:T(8,128)S(1)} %get-tuple-element.26), channel_id=1, source_target_pairs={{0,16},{4,20},{8,24},{12,28},{16,0},{20,4},{24,8},{28,12},{1,17},{... | collective-permute-start | bytes 196616 | tf_op jit(solution)/shard_map/ppermute | solution.py:20
  10.7 7.0 %collective-permute-start.3 = (f32[32,512]{1,0:T(8,128)S(1)}, f32[32,512]{1,0:T(8,128)S(1)}, u32[]{:S(2)}, u32[]{:S(2)}) collective-permute-start(f32[32,512]{1,0:T(8,128)S(1)} %get-tuple-element.27), channel_id=1, source_target_pairs={{0,24},{4,28},{8,16},{12,20},{16,8},{20,12},{24,0},{28,4},{1,25},{... | collective-permute-start | bytes 196616 | tf_op jit(solution)/shard_map/ppermute | solution.py:20
  10.7 11.7 %collective-permute-start.8 = (f32[64,256]{1,0:T(8,128)S(1)}, f32[64,256]{1,0:T(8,128)S(1)}, u32[]{:S(2)}, u32[]{:S(2)}) collective-permute-start(f32[64,256]{1,0:T(8,128)S(1)} %copy-done.1), channel_id=1, source_target_pairs={{0,16},{4,20},{8,24},{12,28},{16,0},{20,4},{24,8},{28,12},{1,17},{... | collective-permute-start | bytes 196616 | tf_op jit(solution)/shard_map/ppermute | solution.py:20
  17.8 5.6 %collective-permute-start.4 = (f32[32,512]{1,0:T(8,128)S(1)}, f32[32,512]{1,0:T(8,128)S(1)}, u32[]{:S(2)}, u32[]{:S(2)}) collective-permute-start(f32[32,512]{1,0:T(8,128)S(1)} %get-tuple-element.29), channel_id=1, source_target_pairs={{0,8},{4,12},{8,0},{12,4},{16,24},{20,28},{24,16},{28,20},{1,9},{5... | collective-permute-start | bytes 196616 | tf_op jit(solution)/shard_map/ppermute | solution.py:20
  19.8 5.4 %collective-permute-start.5 = (f32[32,512]{1,0:T(8,128)S(1)}, f32[32,512]{1,0:T(8,128)S(1)}, u32[]{:S(2)}, u32[]{:S(2)}) collective-permute-start(f32[32,512]{1,0:T(8,128)S(1)} %get-tuple-element.30), channel_id=1, source_target_pairs={{0,16},{4,20},{8,24},{12,28},{16,0},{20,4},{24,8},{28,12},{1,17},{... | collective-permute-start | bytes 196616 | tf_op jit(solution)/shard_map/ppermute | solution.py:20
  21.4 6.1 %collective-permute-start.6 = (f32[32,512]{1,0:T(8,128)S(1)}, f32[32,512]{1,0:T(8,128)S(1)}, u32[]{:S(2)}, u32[]{:S(2)}) collective-permute-start(f32[32,512]{1,0:T(8,128)S(1)} %get-tuple-element.31), channel_id=1, source_target_pairs={{0,24},{4,28},{8,16},{12,20},{16,8},{20,12},{24,0},{28,4},{1,25},{... | collective-permute-start | bytes 196616 | tf_op jit(solution)/shard_map/ppermute | solution.py:20
  22.4 5.3 %collective-permute-start.9 = (f32[64,256]{1,0:T(8,128)S(1)}, f32[64,256]{1,0:T(8,128)S(1)}, u32[]{:S(2)}, u32[]{:S(2)}) collective-permute-start(f32[64,256]{1,0:T(8,128)S(1)} %broadcast_select_fusion), channel_id=1, source_target_pairs={{0,8},{4,12},{8,0},{12,4},{16,24},{20,28},{24,16},{28,20},{1,9},{5... | collective-permute-start | bytes 196616 | tf_op jit(solution)/shard_map/ppermute | solution.py:20
  27.6 11.4 %copy-start = (f32[256,512]{1,0:T(8,128)S(1)}, f32[256,512]{1,0:T(8,128)}, u32[]{:S(2)}) copy-start(f32[256,512]{1,0:T(8,128)} %trailing.3) | copy-start | bytes 1572868
  27.6 15.4 %collective-permute-start.7 = (f32[4,32,512]{2,1,0:T(8,128)S(1)}, f32[4,32,512]{2,1,0:T(8,128)S(1)}, u32[]{:S(2)}, u32[]{:S(2)}) collective-permute-start(f32[4,32,512]{2,1,0:T(8,128)S(1)} %get-tuple-element.32), channel_id=1, source_target_pairs={{0,4},{4,0},{8,12},{12,8},{16,20},{20,16},{24,28},{28,24},{1,5},{5... | collective-permute-start | bytes 786440 | tf_op jit(solution)/shard_map/ppermute | solution.py:20
  27.7 1.6 %collective-permute-start.10 = (f32[64,256]{1,0:T(8,128)S(1)}, f32[64,256]{1,0:T(8,128)S(1)}, u32[]{:S(2)}, u32[]{:S(2)}) collective-permute-start(f32[64,256]{1,0:T(8,128)S(1)} %broadcast_select_fusion.1.diag), channel_id=1, source_target_pairs={{0,4},{4,0},{8,12},{12,8},{16,20},{20,16},{24,28},{28,24},{1,5},{5... | collective-permute-start | bytes 196616 | tf_op jit(solution)/shard_map/ppermute | solution.py:20
  29.3 6.1 %collective-permute-start.11 = (f32[2,64,256]{2,1,0:T(8,128)S(1)}, f32[2,64,256]{2,1,0:T(8,128)S(1)}, u32[]{:S(2)}, u32[]{:S(2)}) collective-permute-start(f32[2,64,256]{2,1,0:T(8,128)S(1)} %shard_map.42.refs_0_), channel_id=1, source_target_pairs={{0,1},{1,0},{2,3},{3,2},{4,5},{5,4},{6,7},{7,6},{8,9},{9,8},{10,11... | collective-permute-start | bytes 393224 | tf_op jit(solution)/shard_map/ppermute | solution.py:20
  30.8 8.1 %collective-permute-start.12 = (f32[2,64,256]{2,1,0:T(8,128)S(1)}, f32[2,64,256]{2,1,0:T(8,128)S(1)}, u32[]{:S(2)}, u32[]{:S(2)}) collective-permute-start(f32[2,64,256]{2,1,0:T(8,128)S(1)} %shard_map.42.refs_0_), channel_id=1, source_target_pairs={{0,2},{1,3},{2,0},{3,1},{4,6},{5,7},{6,4},{7,5},{8,10},{9,11},{10,... | collective-permute-start | bytes 393224 | tf_op jit(solution)/shard_map/ppermute | solution.py:20
  32.4 6.6 %collective-permute-start.13 = (f32[2,64,256]{2,1,0:T(8,128)S(1)}, f32[2,64,256]{2,1,0:T(8,128)S(1)}, u32[]{:S(2)}, u32[]{:S(2)}) collective-permute-start(f32[2,64,256]{2,1,0:T(8,128)S(1)} %shard_map.42.refs_0_), channel_id=1, source_target_pairs={{0,3},{1,2},{2,1},{3,0},{4,7},{5,6},{6,5},{7,4},{8,11},{9,10},{10,... | collective-permute-start | bytes 393224 | tf_op jit(solution)/shard_map/ppermute | solution.py:20

commit v3 on v2

--- a/solution.py
+++ b/solution.py
@@ -9,6 +9,7 @@
 
 VMEM = pl.BlockSpec(memory_space=pltpu.VMEM)
 HBM = pl.BlockSpec(memory_space=pltpu.HBM)
+SMEM = pl.BlockSpec(memory_space=pltpu.SMEM)
 F32 = jnp.float32
 UNROLL = 32
 OUT_PIECES = 2
@@ -45,17 +46,12 @@
     return (rows >= low) & (rows < low + count)
 
 
-def pick_body(given, trailing, keep, send, column, pivots, table, slots, block, sems):
+def pivot_body(given, trailing, slots, table, block, pivots, sems):
     width = pivots.shape[0]
-    rows = trailing.shape[0]
-    lanes = column.shape[1]
-    half = width // 2
-    me = lax.axis_index("prow")
-    core = lax.rem(me, 2)
-    order = pltpu.make_async_copy(given, pivots, sems.at[0])
-    load = pltpu.make_async_copy(trailing, block, sems.at[1])
-    order.start()
+    load = pltpu.make_async_copy(given, pivots, sems.at[0])
     load.start()
+    hold = pltpu.make_async_copy(trailing, block, sems.at[1])
+    hold.start()
 
     def top(i, _):
         for u in range(UNROLL):
@@ -79,31 +75,83 @@
         return 0
 
     lax.fori_loop(0, width // UNROLL, top, 0)
-    order.wait()
+    load.wait()
     lax.fori_loop(0, width // UNROLL, fill, 0)
     lax.fori_loop(0, width // UNROLL, exchange, 0)
-    load.wait()
-
-    def pick(offset, target, index):
+    hold.wait()
+
+
+def pick_body(slots, table, block, beside, column, *pieces):
+    rows, count, size = block.shape[0], len(pieces), pieces[0].shape[0]
+    lanes = column.shape[1]
+    me = lax.axis_index("prow")
+    chip, core = me // 2, lax.rem(me, 2)
+    start = core * count * size
+
+    def pick(index):
+        for d, piece in enumerate(pieces):
+            part = lax.bitwise_xor(chip, d) * size
+            for u in range(size):
+                row = slots[start + part + u]
+                local = index(row)
+                at = pl.ds(local & (rows - 1), 1)
+                own = (local >= rows) == (core == 1)
+                piece[pl.ds(u, 1), :] = jnp.where(own, block[at, :], beside[at, :])
+
+    @pl.when(chip == 0)
+    def _():
+        pick(lambda row: jnp.where(row < 2 * rows, row, table[row]))
+
+    @pl.when(chip != 0)
+    def _():
+        pick(lambda row: row & (2 * rows - 1))
+
+    def ids(i, _):
+        for u in range(UNROLL):
+            j = i * UNROLL + u
+            column[pl.ds(j, 1), :] = jnp.full((1, lanes), slots[start + j], jnp.int32)
+        return 0
+
+    lax.fori_loop(0, column.shape[0] // UNROLL, ids, 0)
+
+
+def rest_body(slots, table, block, beside, column, theirs, tops):
+    rows, half = block.shape[0], column.shape[0]
+    lanes = column.shape[1]
+    me = lax.axis_index("prow")
+    core = lax.rem(me, 2)
+
+    def pick(i, _):
+        for u in range(UNROLL):
+            j = i * UNROLL + u
+            row = slots[(1 - core) * half + j]
+            theirs[pl.ds(j, 1), :] = block[pl.ds(row & (rows - 1), 1), :]
+            column[pl.ds(j, 1), :] = jnp.full((1, lanes), row, jnp.int32)
+        return 0
+
+    lax.fori_loop(0, half // UNROLL, pick, 0)
+
+    def leave(source):
         def some(i, _):
             for u in range(UNROLL):
                 j = i * UNROLL + u
-                row = slots[offset + j]
-                target[pl.ds(j, 1), :] = block[pl.ds(index(row), 1), :]
-                column[pl.ds(offset + j, 1), :] = jnp.full((1, lanes), row, jnp.int32)
+                at = pl.ds(table[slots[core * half + j]], 1)
+                tops[pl.ds(j, 1), :] = source[at, :]
             return 0
 
         lax.fori_loop(0, half // UNROLL, some, 0)
 
     @pl.when(me == 0)
     def _():
-        pick((1 - core) * half, send, lambda row: table[row])
-        pick(core * half, keep, lambda row: table[row])
-
-    @pl.when(me != 0)
+        leave(block)
+
+    @pl.when(me == 1)
     def _():
-        pick((1 - core) * half, send, lambda row: row & (rows - 1))
-        pick(core * half, keep, lambda row: row & (rows - 1))
+        leave(beside)
+
+    @pl.when(me > 1)
+    def _():
+        tops[...] = jnp.zeros_like(tops)
 
 
 def mark_body(column, mark):
@@ -116,21 +164,11 @@
     joined[1] = panel[...]
 
 
-def chip_body(rows, keep, recv, column, *pieces):
-    me = lax.axis_index("prow")
-    chip, core = me // 2, lax.rem(me, 2)
-    for d, piece in enumerate(pieces):
-        part = lax.bitwise_xor(chip, d)
-        ids = column[core * len(pieces) + part][:, 0:1]
-        second = inside(ids, (2 * chip + 1) * rows, rows)
-        piece[...] = jnp.where(second == (core == 1), keep[part], recv[part])
-
-
 def owner_body(rows, count, column, *refs):
     pieces, outs = refs[:count], refs[count:]
     me = lax.axis_index("prow")
-    chip, core = me // 2, lax.rem(me, 2)
-    ids = column[core * count + chip][:, 0:1]
+    chip = me // 2
+    ids = column[chip][:, 0:1]
     holds = [inside(ids, lax.bitwise_xor(chip, d) * 2 * rows, 2 * rows) for d in range(count)]
     chosen = pieces[0][...]
     leaving = pieces[0][...]
@@ -142,19 +180,19 @@
         outs[d][...] = jnp.where(holds[d], leaving, chosen)
 
 
-def share_body(rows, keep, recv, column, *refs):
-    count = keep.shape[0]
-    parts, (own, send) = refs[:count], refs[count:]
-    me = lax.axis_index("prow")
-    chip, core = me // 2, lax.rem(me, 2)
+def share_body(rows, tops, column, *refs):
+    count = tops.shape[0]
+    pieces, parts, (chosen, own, send) = refs[:count], refs[count : 2 * count], refs[2 * count :]
+    me = lax.axis_index("prow")
+    chip = me // 2
     for d in range(count):
         part = lax.bitwise_xor(chip, d)
-        ids = column[core * count + part][:, 0:1]
-        mine, theirs = keep[part], recv[part]
-        second = inside(ids, (2 * chip + 1) * rows, rows)
-        here = jnp.where(second == (core == 1), mine, theirs)
-        there = jnp.where(second & (chip == 0), jnp.where(core == 0, mine, theirs), parts[d][...])
-        own[part] = jnp.where(inside(ids, lax.bitwise_xor(me, 1) * rows, rows), here, there)
+        ids = column[part][:, 0:1]
+        here = pieces[d][...]
+        second = inside(ids, rows, rows) & (chip == 0)
+        there = jnp.where(second, tops[part], parts[d][...])
+        chosen[part] = jnp.where(inside(ids, chip * 2 * rows, 2 * rows), here, there)
+        own[part] = there
         send[part] = jnp.where(inside(ids, me * rows, rows), here, there)
 
 
@@ -202,7 +240,7 @@
     return jnp.concatenate([first, second], axis=0)
 
 
-def factor_body(count, mark, column, trailing, *refs):
+def factor_body(count, mark, mine_ids, their_ids, trailing, *refs):
     del mark
     panels = refs[:count]
     a_ref, sel_ref, base_ref, diag_t, lower_t = refs[count:]
@@ -219,8 +257,9 @@
     j = lax.broadcasted_iota(jnp.int32, (width, rows), 1)
     right = jnp.where(me == 0, (i == j).astype(F32), -lower_t[...])
     a_ref[...] = solve_upper(diag_t[...], right).T
-    ids = column[...].astype(F32).T[0:1, :]
-    own = (me * rows + lax.broadcasted_iota(jnp.int32, (rows, width), 0)).astype(F32)
+    half = mine_ids.shape[0]
+    ids = jnp.concatenate([ref[...].astype(F32).T[0:1, :] for ref in (mine_ids, their_ids)], axis=1)
+    own = (me * rows + lax.broadcasted_iota(jnp.int32, (rows, 2 * half), 0)).astype(F32)
     match = (ids == own) & (me > 0)
     sel = jnp.where(match, 1.0, 0.0)
     sel_ref[...] = sel.astype(jnp.bfloat16)
@@ -228,38 +267,38 @@
     base_ref[...] = jnp.where(drop, 0.0, trailing[...])
 
 
-def update(rows, start, column, picked, arrived, a_ref, sel_ref, at):
-    half = picked.shape[0]
+def update(start, chosen, value, a_ref, sel):
+    half = chosen.shape[0]
     slots = pl.ds(pl.multiple_of(start, half), half)
-    ids = column[slots, 0:1]
-    value = arrived[:, at]
-    chosen = jnp.where(inside(ids, lax.axis_index("prow") * rows, rows), picked[:, at], value)
     high = value.astype(jnp.bfloat16)
     rest = value - high.astype(F32)
     middle = rest.astype(jnp.bfloat16)
     low = (rest - middle.astype(F32)).astype(jnp.bfloat16)
-    sel = sel_ref[:, slots]
     total = dot(a_ref[:, slots], chosen)
     for term in (low, middle, high):
         total += lax.dot(sel, term, preferred_element_type=F32)
     return total
 
 
-def half_body(rows, column, keep, own, a_ref, sel_ref, base, out):
-    half = keep.shape[0]
+def half_body(chosen, own, a_ref, sel_ref, base, out):
+    half = own.shape[0]
     start = lax.rem(lax.axis_index("prow"), 2) * half
-    out[...] = base[...] + update(rows, start, column, keep, own, a_ref, sel_ref, slice(None))
-
-
-def finish_body(rows, column, send, recv, a_ref, sel_ref, partial, out, block, sems):
-    half = send.shape[0]
-    start = (1 - lax.rem(lax.axis_index("prow"), 2)) * half
+    out[...] = base[...] + update(start, chosen[...], own[...], a_ref, sel_ref[:, :half])
+
+
+def finish_body(rows, ids, theirs, recv, a_ref, sel_ref, partial, out, block, sems):
+    half = recv.shape[0]
+    me = lax.axis_index("prow")
+    start = (1 - lax.rem(me, 2)) * half
     pieces = sems.shape[0]
     width = out.shape[1] // pieces
+    mine = inside(ids[:, 0:1], me * rows, rows)
     copies = []
     for k in range(pieces):
         at = slice(k * width, (k + 1) * width)
-        block[:, at] = partial[:, at] + update(rows, start, column, send, recv, a_ref, sel_ref, at)
+        value = recv[:, at]
+        chosen = jnp.where(mine, theirs[:, at], value)
+        block[:, at] = partial[:, at] + update(start, chosen, value, a_ref, sel_ref[:, half:])
         copies.append(pltpu.make_async_copy(block.at[:, at], out.at[:, at], sems.at[k]))
         copies[-1].start()
     for copy in copies:
@@ -280,20 +319,40 @@
     def array(*shape, dtype=F32):
         return pltpu.VMEM(shape, dtype)
 
-    keep, send, column = call(
-        pick_body,
-        (array(half, cols), array(half, cols), array(width, 128, dtype=jnp.int32)),
+    beside = pair_exchange(trailing_in, "prow", 1)
+    slots, table, block = call(
+        pivot_body,
+        (
+            pltpu.SMEM((width,), jnp.int32),
+            pltpu.SMEM((rows * devices,), jnp.int32),
+            array(rows, cols),
+        ),
         pivots,
         trailing_in,
         in_specs=(HBM, HBM),
-        scratch=(
-            pltpu.SMEM((width,), jnp.int32),
-            pltpu.SMEM((rows * devices,), jnp.int32),
-            pltpu.SMEM((width,), jnp.int32),
-            pltpu.VMEM((rows, cols), F32),
-            pltpu.SemaphoreType.DMA((2,)),
-        ),
-    )
+        out_specs=(SMEM, SMEM, VMEM),
+        scratch=(pltpu.SMEM((width,), jnp.int32), pltpu.SemaphoreType.DMA((2,))),
+    )
+    scalars = (SMEM, SMEM, VMEM, VMEM)
+    column, *pieces = call(
+        pick_body,
+        [array(half, 128, dtype=jnp.int32)] + [array(size, cols)] * chips,
+        slots,
+        table,
+        block,
+        beside,
+        in_specs=scalars,
+    )
+    others, theirs, tops = call(
+        rest_body,
+        (array(half, 128, dtype=jnp.int32), array(half, cols), array(half, cols)),
+        slots,
+        table,
+        block,
+        beside,
+        in_specs=scalars,
+    )
+    ids = column.reshape(chips, size, 128)
     me = lax.axis_index("prow")
     diag, arrived, bit = panel_t, panel_t, devices // 2
     while bit:
@@ -305,19 +364,20 @@
     (joined,) = call(join_body, (array(2, depth, rows),), mark, panel_t, diag, arrived)
     panels = [joined] + [pair_exchange(joined, "pcol", d) for d in range(1, spread)]
 
-    recv = pair_exchange(send, "prow", 1).reshape(chips, size, cols)
-    cut = keep.reshape(chips, size, cols)
-    ids = column.reshape(devices, size, 128)
-    pieces = call(functools.partial(chip_body, rows), [array(size, cols)] * chips, cut, recv, ids)
     gathered = [pieces[0]] + [pair_exchange(pieces[d], "prow", 2 * d) for d in range(1, chips)]
     parts = call(
         functools.partial(owner_body, rows, chips), [array(size, cols)] * chips, ids, *gathered
     )
     parts = [parts[0]] + [pair_exchange(parts[d], "prow", 2 * d) for d in range(1, chips)]
-    own, other = call(
-        functools.partial(share_body, rows), [array(chips, size, cols)] * 2, cut, recv, ids, *parts
-    )
-    own = own.reshape(half, cols)
+    chosen, own, other = call(
+        functools.partial(share_body, rows),
+        [array(chips, size, cols)] * 3,
+        tops.reshape(chips, size, cols),
+        ids,
+        *pieces,
+        *parts,
+    )
+    chosen, own = chosen.reshape(half, cols), own.reshape(half, cols)
     arrived = pair_exchange(other, "prow", 1).reshape(half, cols)
     (mark,) = call(mark_body, (array(8, 128, dtype=jnp.int32),), column)
     a, sel, base = call(
@@ -325,18 +385,17 @@
         (array(rows, width), array(rows, width, dtype=jnp.bfloat16), array(rows, cols)),
         mark,
         column,
-        trailing_in,
+        others,
+        block,
         *panels,
         scratch=(pltpu.VMEM((width, width), F32), pltpu.VMEM((width, rows), F32)),
     )
-    (partial,) = call(
-        functools.partial(half_body, rows), (array(rows, cols),), column, keep, own, a, sel, base
-    )
+    (partial,) = call(half_body, (array(rows, cols),), chosen, own, a, sel, base)
     (out,) = call(
         functools.partial(finish_body, rows),
         (jax.ShapeDtypeStruct((rows, cols), F32),),
-        column,
-        send,
+        others,
+        theirs,
         arrived,
         a,
         sel,

time: 44.6 us -> 42.8 us (0.960)
  waiting for transfers between devices: 17.5 us -> 14.7 us
  Pallas kernels: 9.06 us -> 9.83 us
    ppermute x14, waiting for transfers between devices: 17.5 us -> 14.7 us  [pair_exchange(): return lax.ppermute(value, axis, [(i, i ^ bit) for i in range(size)])]
    pallas_call x9 -> x10, Pallas kernels: 9.06 us -> 9.83 us  [kernel(): pl.pallas_call(body, out_shape=tuple(outs), in_specs=list(in_specs), out_...]
  transfers between devices with their start and end apart: 14 -> 14, of which waited for: 7 -> 7; matrix products, arithmetic and copies ran while one was open for 0% -> 0% of each run, Pallas kernels for 9% -> 17%
where the time goes in v3:
time: 42.8 us; the launch traced here: 42.7 us
  starting transfers between devices  18 us (42%)
  waiting for transfers between devices  14.7 us (34%)
  Pallas kernels  9.83 us (23%)
    ppermute x14, starting transfers between devices, pair_exchange(): return lax.ppermute(value, axis, [(i, i ^ bit) for i in range(size)])  18 us
    ppermute x14, waiting for transfers between devices, pair_exchange(): return lax.ppermute(value, axis, [(i, i ^ bit) for i in range(size)])  14.7 us
    pallas_call x10, Pallas kernels, kernel(): pl.pallas_call(body, out_shape=tuple(outs), in_specs=list(in_specs), out_...  9.83 us
  transfers between devices with their start and end apart: 14, of which 7 were waited for; matrix products, arithmetic and copies ran while one was open for 0% of the time, Pallas kernels for 17%

profile of v3, /device:TPU:0, one launch (start us, length us, event | category | flops | bytes accessed | tf_op | source)
XLA Modules:
  0.0 42.7 jit_solution(12440227441605798778)
XLA Ops:
  0.0 0.5 %collective-permute-start = (f32[256,512]{1,0:T(8,128)}, f32[256,512]{1,0:T(8,128)S(1)}, u32[]{:S(2)}, u32[]{:S(2)}) collective-permute-start(f32[256,512]{1,0:T(8,128)} %trailing.1), channel_id=1, source_target_pairs={{0,4},{4,0},{8,12},{12,8},{16,20},{20,16},{24,28},{28,24},{1,5},{5... | collective-permute-start | bytes 1572872 | tf_op jit(solution)/shard_map/ppermute | solution.py:21
  0.5 2.2 %shard_map.37 = (s32[256]{0:T(256)S(4)}, s32[2048]{0:T(1024)S(4)}, f32[256,512]{1,0:T(8,128)S(1)}) custom-call(s32[256]{0:T(256)} %given.1, f32[256,512]{1,0:T(8,128)} %trailing.1), custom_call_target="tpu_custom_call" | custom-call | tf_op jit(solution)/shard_map/pallas_call | solution.py:35
  2.7 0.9 %shard_map.39 = (s32[128,128]{1,0:T(8,128)S(1)}, f32[32,512]{1,0:T(8,128)S(1)}, f32[32,512]{1,0:T(8,128)S(1)}, f32[32,512]{1,0:T(8,128)S(1)}, f32[32,512]{1,0:T(8,128)S(1)}) custom-call(s32[256]{0:T(256)S(4)} %get-tuple-element.26.slots, s32[2048]{0:T(1024)S(4)} %get-tuple-element.27.table, f32[256,512]{1,0:T(8,128)S(1)} %get-tuple-element.28.block.trailing, ...), custom_call_target="tpu_custom_call" | custom-call | tf_op jit(solution)/shard_map/pallas_call | solution.py:35
  3.6 2.6 %collective-permute-start.1 = (f32[32,512]{1,0:T(8,128)S(1)}, f32[32,512]{1,0:T(8,128)S(1)}, u32[]{:S(2)}, u32[]{:S(2)}) collective-permute-start(f32[32,512]{1,0:T(8,128)S(1)} %get-tuple-element.34.refs_1_), channel_id=1, source_target_pairs={{0,8},{4,12},{8,0},{12,4},{16,24},{20,28},{24,16},{28,20},{1,9},{5... | collective-permute-start | bytes 196616 | tf_op jit(solution)/shard_map/ppermute | solution.py:21
  6.2 2.6 %collective-permute-start.2 = (f32[32,512]{1,0:T(8,128)S(1)}, f32[32,512]{1,0:T(8,128)S(1)}, u32[]{:S(2)}, u32[]{:S(2)}) collective-permute-start(f32[32,512]{1,0:T(8,128)S(1)} %get-tuple-element.35.refs_2_), channel_id=1, source_target_pairs={{0,16},{4,20},{8,24},{12,28},{16,0},{20,4},{24,8},{28,12},{1,17},{... | collective-permute-start | bytes 196616 | tf_op jit(solution)/shard_map/ppermute | solution.py:21
  8.8 1.9 %collective-permute-start.8 = (f32[64,256]{1,0:T(8,128)S(1)}, f32[64,256]{1,0:T(8,128)S(1)}, u32[]{:S(2)}, u32[]{:S(2)}) collective-permute-start(f32[64,256]{1,0:T(8,128)S(1)} %copy-done), channel_id=1, source_target_pairs={{0,16},{4,20},{8,24},{12,28},{16,0},{20,4},{24,8},{28,12},{1,17},{... | collective-permute-start | bytes 196616 | tf_op jit(solution)/shard_map/ppermute | solution.py:21
  10.7 2.5 %collective-permute-done.2.refs_2_ = f32[32,512]{1,0:T(8,128)S(1)} collective-permute-done((f32[32,512]{1,0:T(8,128)S(1)}, f32[32,512]{1,0:T(8,128)S(1)}, u32[]{:S(2)}, u32[]{:S(2)}) %collective-permute-start.2) | collective-permute-done | bytes 65568 | tf_op jit(solution)/shard_map/ppermute | solution.py:21
  13.2 2.1 %collective-permute-done.3.refs_3_ = f32[32,512]{1,0:T(8,128)S(1)} collective-permute-done((f32[32,512]{1,0:T(8,128)S(1)}, f32[32,512]{1,0:T(8,128)S(1)}, u32[]{:S(2)}, u32[]{:S(2)}) %collective-permute-start.3) | collective-permute-done | bytes 65568 | tf_op jit(solution)/shard_map/ppermute | solution.py:21
  15.4 2.7 %collective-permute-start.4 = (f32[32,512]{1,0:T(8,128)S(1)}, f32[32,512]{1,0:T(8,128)S(1)}, u32[]{:S(2)}, u32[]{:S(2)}) collective-permute-start(f32[32,512]{1,0:T(8,128)S(1)} %get-tuple-element.38), channel_id=1, source_target_pairs={{0,8},{4,12},{8,0},{12,4},{16,24},{20,28},{24,16},{28,20},{1,9},{5... | collective-permute-start | bytes 196616 | tf_op jit(solution)/shard_map/ppermute | solution.py:21
  18.1 1.4 %collective-permute-start.5 = (f32[32,512]{1,0:T(8,128)S(1)}, f32[32,512]{1,0:T(8,128)S(1)}, u32[]{:S(2)}, u32[]{:S(2)}) collective-permute-start(f32[32,512]{1,0:T(8,128)S(1)} %get-tuple-element.39), channel_id=1, source_target_pairs={{0,16},{4,20},{8,24},{12,28},{16,0},{20,4},{24,8},{28,12},{1,17},{... | collective-permute-start | bytes 196616 | tf_op jit(solution)/shard_map/ppermute | solution.py:21
  19.5 1.4 %collective-permute-start.6 = (f32[32,512]{1,0:T(8,128)S(1)}, f32[32,512]{1,0:T(8,128)S(1)}, u32[]{:S(2)}, u32[]{:S(2)}) collective-permute-start(f32[32,512]{1,0:T(8,128)S(1)} %get-tuple-element.40), channel_id=1, source_target_pairs={{0,24},{4,28},{8,16},{12,20},{16,8},{20,12},{24,0},{28,4},{1,25},{... | collective-permute-start | bytes 196616 | tf_op jit(solution)/shard_map/ppermute | solution.py:21
  20.9 0.8 %collective-permute-start.9 = (f32[64,256]{1,0:T(8,128)S(1)}, f32[64,256]{1,0:T(8,128)S(1)}, u32[]{:S(2)}, u32[]{:S(2)}) collective-permute-start(f32[64,256]{1,0:T(8,128)S(1)} %broadcast_select_fusion), channel_id=1, source_target_pairs={{0,8},{4,12},{8,0},{12,4},{16,24},{20,28},{24,16},{28,20},{1,9},{5... | collective-permute-start | bytes 196616 | tf_op jit(solution)/shard_map/ppermute | solution.py:21
  21.7 1.1 %shard_map.38 = (s32[128,128]{1,0:T(8,128)S(1)}, f32[128,512]{1,0:T(8,128)S(1)}, f32[128,512]{1,0:T(8,128)S(1)}) custom-call(s32[256]{0:T(256)S(4)} %get-tuple-element.26.slots, s32[2048]{0:T(1024)S(4)} %get-tuple-element.27.table, f32[256,512]{1,0:T(8,128)S(1)} %get-tuple-element.28.block.trailing, f32[256,512]{1,0:T(8,128)S(1)} %collective-permute-done.beside), custom_call_target="tpu_custom_call" | custom-call | tf_op jit(solution)/shard_map/pallas_call | solution.py:35
  22.8 1.4 %collective-permute-done.5.refs_6_ = f32[32,512]{1,0:T(8,128)S(1)} collective-permute-done((f32[32,512]{1,0:T(8,128)S(1)}, f32[32,512]{1,0:T(8,128)S(1)}, u32[]{:S(2)}, u32[]{:S(2)}) %collective-permute-start.5) | collective-permute-done | bytes 65568 | tf_op jit(solution)/shard_map/ppermute | solution.py:21
  24.2 1.4 %collective-permute-done.6.refs_7_ = f32[32,512]{1,0:T(8,128)S(1)} collective-permute-done((f32[32,512]{1,0:T(8,128)S(1)}, f32[32,512]{1,0:T(8,128)S(1)}, u32[]{:S(2)}, u32[]{:S(2)}) %collective-permute-start.6) | collective-permute-done | bytes 65568 | tf_op jit(solution)/shard_map/ppermute | solution.py:21
  25.9 0.5 %collective-permute-start.10 = (f32[64,256]{1,0:T(8,128)S(1)}, f32[64,256]{1,0:T(8,128)S(1)}, u32[]{:S(2)}, u32[]{:S(2)}) collective-permute-start(f32[64,256]{1,0:T(8,128)S(1)} %broadcast_select_fusion.1.diag), channel_id=1, source_target_pairs={{0,4},{4,0},{8,12},{12,8},{16,20},{20,16},{24,28},{28,24},{1,5},{5... | collective-permute-start | bytes 196616 | tf_op jit(solution)/shard_map/ppermute | solution.py:21
  26.4 1.0 %collective-permute-done.10.arrived = f32[64,256]{1,0:T(8,128)S(1)} collective-permute-done((f32[64,256]{1,0:T(8,128)S(1)}, f32[64,256]{1,0:T(8,128)S(1)}, u32[]{:S(2)}, u32[]{:S(2)}) %collective-permute-start.10) | collective-permute-done | bytes 65568 | tf_op jit(solution)/shard_map/ppermute | solution.py:21
  27.5 1.6 %collective-permute-start.11 = (f32[2,64,256]{2,1,0:T(8,128)S(1)}, f32[2,64,256]{2,1,0:T(8,128)S(1)}, u32[]{:S(2)}, u32[]{:S(2)}) collective-permute-start(f32[2,64,256]{2,1,0:T(8,128)S(1)} %shard_map.43.refs_0_), channel_id=1, source_target_pairs={{0,1},{1,0},{2,3},{3,2},{4,5},{5,4},{6,7},{7,6},{8,9},{9,8},{10,11... | collective-permute-start | bytes 393224 | tf_op jit(solution)/shard_map/ppermute | solution.py:21
  29.1 1.5 %collective-permute-start.12 = (f32[2,64,256]{2,1,0:T(8,128)S(1)}, f32[2,64,256]{2,1,0:T(8,128)S(1)}, u32[]{:S(2)}, u32[]{:S(2)}) collective-permute-start(f32[2,64,256]{2,1,0:T(8,128)S(1)} %shard_map.43.refs_0_), channel_id=1, source_target_pairs={{0,2},{1,3},{2,0},{3,1},{4,6},{5,7},{6,4},{7,5},{8,10},{9,11},{10,... | collective-permute-start | bytes 393224 | tf_op jit(solution)/shard_map/ppermute | solution.py:21
  31.1 2.5 %collective-permute-done.11.refs_1_ = f32[2,64,256]{2,1,0:T(8,128)S(1)} collective-permute-done((f32[2,64,256]{2,1,0:T(8,128)S(1)}, f32[2,64,256]{2,1,0:T(8,128)S(1)}, u32[]{:S(2)}, u32[]{:S(2)}) %collective-permute-start.11) | collective-permute-done | bytes 131104 | tf_op jit(solution)/shard_map/ppermute | solution.py:21
  33.6 3.6 %collective-permute-done.12.refs_2_ = f32[2,64,256]{2,1,0:T(8,128)S(1)} collective-permute-done((f32[2,64,256]{2,1,0:T(8,128)S(1)}, f32[2,64,256]{2,1,0:T(8,128)S(1)}, u32[]{:S(2)}, u32[]{:S(2)}) %collective-permute-start.12) | collective-permute-done | bytes 131104 | tf_op jit(solution)/shard_map/ppermute | solution.py:21
  37.2 3.1 %shard_map.44 = (f32[256,256]{1,0:T(8,128)S(1)}, bf16[256,256]{1,0:T(8,128)(2,1)S(1)}, f32[256,512]{1,0:T(8,128)S(1)}) custom-call(s32[8,128]{1,0:T(8,128)S(1)} %shard_map.42.mark, s32[128,128]{1,0:T(8,128)S(1)} %get-tuple-element.32.column.mine_ids, s32[128,128]{1,0:T(8,128)S(1)} %get-tuple-element.29.their_ids.ids, ...), custom_call_target="tpu_custom_call" | custom-call | tf_op jit(solution)/shard_map/pallas_call | solution.py:35
  40.3 0.8 %shard_map.45.partial = f32[256,512]{1,0:T(8,128)S(1)} custom-call(f32[128,512]{1,0:T(8,128)S(1)} %bitcast.7, f32[128,512]{1,0:T(8,128)S(1)} %bitcast.8, f32[256,256]{1,0:T(8,128)S(1)} %get-tuple-element.42.a_ref, bf16[256,256]{1,0:T(8,128)(2,1)S(1)} %get-tuple-element.43.sel_ref, f32[256,512]{1,0:T(8,128)S(1)} %get-tuple-element.46.base), custom_call_target="tpu_custom_call" | custom-call | tf_op jit(solution)/shard_map/pallas_call | solution.py:35
  41.1 1.5 %shard_map.46 = f32[256,512]{1,0:T(8,128)} custom-call(s32[128,128]{1,0:T(8,128)S(1)} %get-tuple-element.29.their_ids.ids, f32[128,512]{1,0:T(8,128)S(1)} %get-tuple-element.30.theirs, f32[128,512]{1,0:T(8,128)S(1)} %bitcast.10, f32[256,256]{1,0:T(8,128)S(1)} %get-tuple-element.42.a_ref, bf16[256,256]{1,0:T(8,128)(2,1)S(1)} %get-tuple-element.43.sel_ref, ...), custom_call_target="tpu_custom_call" | custom-call | tf_op jit(solution)/shard_map/pallas_call | solution.py:35
  (18 shorter events, 0.9 us)
Async XLA Ops:
  0.0 2.7 %collective-permute-start = (f32[256,512]{1,0:T(8,128)}, f32[256,512]{1,0:T(8,128)S(1)}, u32[]{:S(2)}, u32[]{:S(2)}) collective-permute-start(f32[256,512]{1,0:T(8,128)} %trailing.1), channel_id=1, source_target_pairs={{0,4},{4,0},{8,12},{12,8},{16,20},{20,16},{24,28},{28,24},{1,5},{5... | collective-permute-start | bytes 1572872 | tf_op jit(solution)/shard_map/ppermute | solution.py:21
  2.7 6.0 %copy-start = (f32[64,256]{1,0:T(8,128)S(1)}, f32[64,256]{1,0:T(8,128)}, u32[]{:S(2)}) copy-start(f32[64,256]{1,0:T(8,128)} %panel.1) | copy-start | bytes 196612
  3.6 7.1 %collective-permute-start.1 = (f32[32,512]{1,0:T(8,128)S(1)}, f32[32,512]{1,0:T(8,128)S(1)}, u32[]{:S(2)}, u32[]{:S(2)}) collective-permute-start(f32[32,512]{1,0:T(8,128)S(1)} %get-tuple-element.34.refs_1_), channel_id=1, source_target_pairs={{0,8},{4,12},{8,0},{12,4},{16,24},{20,28},{24,16},{28,20},{1,9},{5... | collective-permute-start | bytes 196616 | tf_op jit(solution)/shard_map/ppermute | solution.py:21
  6.2 7.0 %collective-permute-start.2 = (f32[32,512]{1,0:T(8,128)S(1)}, f32[32,512]{1,0:T(8,128)S(1)}, u32[]{:S(2)}, u32[]{:S(2)}) collective-permute-start(f32[32,512]{1,0:T(8,128)S(1)} %get-tuple-element.35.refs_2_), channel_id=1, source_target_pairs={{0,16},{4,20},{8,24},{12,28},{16,0},{20,4},{24,8},{28,12},{1,17},{... | collective-permute-start | bytes 196616 | tf_op jit(solution)/shard_map/ppermute | solution.py:21
  8.8 6.5 %collective-permute-start.3 = (f32[32,512]{1,0:T(8,128)S(1)}, f32[32,512]{1,0:T(8,128)S(1)}, u32[]{:S(2)}, u32[]{:S(2)}) collective-permute-start(f32[32,512]{1,0:T(8,128)S(1)} %get-tuple-element.36.refs_3_), channel_id=1, source_target_pairs={{0,24},{4,28},{8,16},{12,20},{16,8},{20,12},{24,0},{28,4},{1,25},{... | collective-permute-start | bytes 196616 | tf_op jit(solution)/shard_map/ppermute | solution.py:21
  8.8 12.1 %collective-permute-start.8 = (f32[64,256]{1,0:T(8,128)S(1)}, f32[64,256]{1,0:T(8,128)S(1)}, u32[]{:S(2)}, u32[]{:S(2)}) collective-permute-start(f32[64,256]{1,0:T(8,128)S(1)} %copy-done), channel_id=1, source_target_pairs={{0,16},{4,20},{8,24},{12,28},{16,0},{20,4},{24,8},{28,12},{1,17},{... | collective-permute-start | bytes 196616 | tf_op jit(solution)/shard_map/ppermute | solution.py:21
  15.4 7.3 %collective-permute-start.4 = (f32[32,512]{1,0:T(8,128)S(1)}, f32[32,512]{1,0:T(8,128)S(1)}, u32[]{:S(2)}, u32[]{:S(2)}) collective-permute-start(f32[32,512]{1,0:T(8,128)S(1)} %get-tuple-element.38), channel_id=1, source_target_pairs={{0,8},{4,12},{8,0},{12,4},{16,24},{20,28},{24,16},{28,20},{1,9},{5... | collective-permute-start | bytes 196616 | tf_op jit(solution)/shard_map/ppermute | solution.py:21
  18.1 6.1 %collective-permute-start.5 = (f32[32,512]{1,0:T(8,128)S(1)}, f32[32,512]{1,0:T(8,128)S(1)}, u32[]{:S(2)}, u32[]{:S(2)}) collective-permute-start(f32[32,512]{1,0:T(8,128)S(1)} %get-tuple-element.39), channel_id=1, source_target_pairs={{0,16},{4,20},{8,24},{12,28},{16,0},{20,4},{24,8},{28,12},{1,17},{... | collective-permute-start | bytes 196616 | tf_op jit(solution)/shard_map/ppermute | solution.py:21
  19.5 6.2 %collective-permute-start.6 = (f32[32,512]{1,0:T(8,128)S(1)}, f32[32,512]{1,0:T(8,128)S(1)}, u32[]{:S(2)}, u32[]{:S(2)}) collective-permute-start(f32[32,512]{1,0:T(8,128)S(1)} %get-tuple-element.40), channel_id=1, source_target_pairs={{0,24},{4,28},{8,16},{12,20},{16,8},{20,12},{24,0},{28,4},{1,25},{... | collective-permute-start | bytes 196616 | tf_op jit(solution)/shard_map/ppermute | solution.py:21
  20.9 5.0 %collective-permute-start.9 = (f32[64,256]{1,0:T(8,128)S(1)}, f32[64,256]{1,0:T(8,128)S(1)}, u32[]{:S(2)}, u32[]{:S(2)}) collective-permute-start(f32[64,256]{1,0:T(8,128)S(1)} %broadcast_select_fusion), channel_id=1, source_target_pairs={{0,8},{4,12},{8,0},{12,4},{16,24},{20,28},{24,16},{28,20},{1,9},{5... | collective-permute-start | bytes 196616 | tf_op jit(solution)/shard_map/ppermute | solution.py:21
  25.8 15.3 %collective-permute-start.7 = (f32[4,32,512]{2,1,0:T(8,128)S(1)}, f32[4,32,512]{2,1,0:T(8,128)S(1)}, u32[]{:S(2)}, u32[]{:S(2)}) collective-permute-start(f32[4,32,512]{2,1,0:T(8,128)S(1)} %get-tuple-element.41), channel_id=1, source_target_pairs={{0,4},{4,0},{8,12},{12,8},{16,20},{20,16},{24,28},{28,24},{1,5},{5... | collective-permute-start | bytes 786440 | tf_op jit(solution)/shard_map/ppermute | solution.py:21
  25.9 1.6 %collective-permute-start.10 = (f32[64,256]{1,0:T(8,128)S(1)}, f32[64,256]{1,0:T(8,128)S(1)}, u32[]{:S(2)}, u32[]{:S(2)}) collective-permute-start(f32[64,256]{1,0:T(8,128)S(1)} %broadcast_select_fusion.1.diag), channel_id=1, source_target_pairs={{0,4},{4,0},{8,12},{12,8},{16,20},{20,16},{24,28},{28,24},{1,5},{5... | collective-permute-start | bytes 196616 | tf_op jit(solution)/shard_map/ppermute | solution.py:21
  27.5 6.1 %collective-permute-start.11 = (f32[2,64,256]{2,1,0:T(8,128)S(1)}, f32[2,64,256]{2,1,0:T(8,128)S(1)}, u32[]{:S(2)}, u32[]{:S(2)}) collective-permute-start(f32[2,64,256]{2,1,0:T(8,128)S(1)} %shard_map.43.refs_0_), channel_id=1, source_target_pairs={{0,1},{1,0},{2,3},{3,2},{4,5},{5,4},{6,7},{7,6},{8,9},{9,8},{10,11... | collective-permute-start | bytes 393224 | tf_op jit(solution)/shard_map/ppermute | solution.py:21
  29.1 8.1 %collective-permute-start.12 = (f32[2,64,256]{2,1,0:T(8,128)S(1)}, f32[2,64,256]{2,1,0:T(8,128)S(1)}, u32[]{:S(2)}, u32[]{:S(2)}) collective-permute-start(f32[2,64,256]{2,1,0:T(8,128)S(1)} %shard_map.43.refs_0_), channel_id=1, source_target_pairs={{0,2},{1,3},{2,0},{3,1},{4,6},{5,7},{6,4},{7,5},{8,10},{9,11},{10,... | collective-permute-start | bytes 393224 | tf_op jit(solution)/shard_map/ppermute | solution.py:21
  30.6 6.6 %collective-permute-start.13 = (f32[2,64,256]{2,1,0:T(8,128)S(1)}, f32[2,64,256]{2,1,0:T(8,128)S(1)}, u32[]{:S(2)}, u32[]{:S(2)}) collective-permute-start(f32[2,64,256]{2,1,0:T(8,128)S(1)} %shard_map.43.refs_0_), channel_id=1, source_target_pairs={{0,3},{1,2},{2,1},{3,0},{4,7},{5,6},{6,5},{7,4},{8,11},{9,10},{10,... | collective-permute-start | bytes 393224 | tf_op jit(solution)/shard_map/ppermute | solution.py:21
